TPU v7x, 512 devices: a whole 4x4x16 slice. The times are simulated.
512 devices in a mesh: row: 32 (over z, core), col: 16 (over x, y).
Axes of the slice: x: 4, y: 4, z: 16, core: 2. Of those that a mesh axis runs over, the one named last changes fastest.
Arguments:
- slab: float32 [16384, 4096], P('row', 'col'), may hold values from -6 to 6
- panels: float32 [3, 16384, 512], P(None, 'row', 'col'), may hold values from -0.125 to 0.125
- pivots: int32 [3, 512], replicated, may hold values from 0 to 16383, as said below
Outputs:
- updated_slab: float32 [16384, 4096], P('row', 'col')
Inputs may be any that keep to these rules, and one draw needn't show every extreme that they name: Each pivots[k, i] is either k * 512 + i or a row at or below (k + 1) * 512; the rows of one panel are distinct.
All inputs are finite; a program needn't handle non-finite values.
Results may differ from a plain program's by a relative error of at most 0.0001.
Values sent between devices are 32-bit elements; how exact they have to be, the bound alone decides.
A program may use at most 64 MiB of HBM per device.

v0:
```python
import jax
import jax.numpy as jnp
from jax import lax
from jax.sharding import PartitionSpec as P


def spread(block, axis, holder):
    block = jnp.where(lax.axis_index(axis) == holder, block, jnp.zeros_like(block))
    return lax.psum(block, axis)


def forward_solve(unit_lower, rhs):
    return lax.linalg.triangular_solve(
        unit_lower, rhs, left_side=True, lower=True, unit_diagonal=True
    )


def local(slab, panels, pivots):
    rows, cols = slab.shape
    ticks, width = pivots.shape
    first_row = lax.axis_index("row") * rows
    global_rows = first_row + jnp.arange(rows, dtype=jnp.int32)
    for tick in range(ticks):
        panel = lax.all_gather(panels[tick], "col", axis=1, tiled=True)
        top_start = tick * width
        top_end = top_start + width
        old_parts = []
        lower_parts = []
        for owner in range(top_start // rows, (top_end - 1) // rows + 1):
            low = max(top_start, owner * rows) - owner * rows
            high = min(top_end, (owner + 1) * rows) - owner * rows
            got_rows, got_panel = (spread(slab, "row", owner), spread(panel, "row", owner))
            old_parts.append(got_rows)
            lower_parts.append(got_panel)
        old_top = old_parts[0]
        panel_top = lower_parts[0]
        unit_lower = jnp.tril(panel_top, -1) + jnp.eye(width, dtype=jnp.float32)
        sources = pivots[tick]
        top_ids = top_start + jnp.arange(width, dtype=jnp.int32)
        moved = sources != top_ids
        local_ids = sources - first_row
        inside = (local_ids >= 0) & (local_ids < rows)
        picked = jnp.take(slab, jnp.clip(local_ids, 0, rows - 1), axis=0)
        offered = jnp.where(inside[:, None], picked, jnp.float32(0.0))
        new_top = lax.psum(offered, "row")
        upper = forward_solve(unit_lower, new_top)
        matches = (sources[None, :] == global_rows[:, None]) & moved[None, :]
        incoming = jnp.dot(
            matches.astype(jnp.float32),
            old_top,
            precision=lax.Precision.HIGHEST,
            preferred_element_type=jnp.float32,
        )
        swapped = jnp.where(jnp.any(matches, axis=1)[:, None], incoming, slab)
        in_top = (global_rows >= top_start) & (global_rows < top_end)
        top_local = jnp.take(upper, jnp.clip(global_rows - top_start, 0, width - 1), axis=0)
        lowered = swapped - jnp.dot(
            panel, upper, precision=lax.Precision.HIGHEST, preferred_element_type=jnp.float32
        )
        below = global_rows >= top_end
        slab = jnp.where(below[:, None], lowered, jnp.where(in_top[:, None], top_local, swapped))
    return slab


def solution(mesh):
    in_specs = (P("row", "col"), P(None, "row", "col"), P())
    out_specs = P("row", "col")
    return jax.shard_map(local, mesh=mesh, in_specs=in_specs, out_specs=out_specs, check_vma=False)
```

profile of v0, /device:TPU:1, one launch (start us, length us, event | category | flops | bytes accessed | tf_op | source)
XLA Modules:
  0.0 970.3 jit_solution(11171664072157518661)
XLA Ops:
  9.7 1.6 gather_fusion
  12.5 59.2 %all-gather.7.cloned.1.call-done = f32[1,512,512]{1,0,2:T(1,128)} async-done(((f32[1,512,32]{1,0,2:T(1,128)}), f32[1,512,512]{1,0,2:T(1,128)}) %all-gather.7.cloned.1.call-update) | async-done | bytes 1048592 | tf_op jit(solution)/shard_map/all_gather | solution.py:24
  71.7 2.3 bitcast_select_fusion.2
  75.6 56.4 %all-gather.9.cloned.1.call-done = f32[1,512,512]{1,0,2:T(1,128)} async-done(((f32[1,512,32]{1,0,2:T(1,128)}), f32[1,512,512]{1,0,2:T(1,128)}) %all-gather.9.cloned.1.call-update) | async-done | bytes 1048592 | tf_op jit(solution)/shard_map/all_gather | solution.py:24
  131.9 2.3 bitcast_select_fusion.1
  134.2 217.6 %all-reduce.11.cloned.1.call-done = (f32[512,256]{1,0:T(8,128)}, f32[512,256]{1,0:T(8,128)}, f32[512,512]{0,1:T(8,128)}) async-done(((f32[512,256]{1,0:T(8,128)}, f32[512,256]{1,0:T(8,128)}, f32[512,512]{0,1:T(8,128)}), (f32[512,256]{1,0:T(8,128)}, f32[512,256]{1,0:T(8,128)}, f32[512,512]{0,1:T(8,128)})) %all-reduce.11.cloned.1.call-update) | async-done | bytes 2097168 | tf_op jit(solution)/shard_map/psum | solution.py:9
  351.8 1.4 convert_add_fusion.2
  353.3 8.8 while.6
  354.0 1.4 dynamic-slice.17
  356.2 1.4 dynamic-slice.17
  358.4 1.4 dynamic-slice.17
  360.6 1.4 dynamic-slice.17
  362.1 39.3 %custom-call.5 = f32[4,128,128]{1,2,0:T(8,128)S(1)} custom-call(f32[4,128,128]{2,1,0:T(8,128)S(1)} %get-tuple-element.27), custom_call_target="InvertDiagBlocksLowerTriangular" | custom-call | tf_op jit(solution)/shard_map/triangular_solve/custom-call.1 | solution.py:13
  404.0 1.6 gather_fusion.1
  406.8 2.7 broadcast_select_fusion.1
  409.5 1.6 gather_fusion.2
  412.5 2.3 bitcast_select_fusion
  414.8 215.5 %all-reduce.9.cloned.1.call-done = (f32[512,256]{1,0:T(8,128)}, f32[512,256]{1,0:T(8,128)}, f32[512,512]{0,1:T(8,128)}) async-done(((f32[512,256]{1,0:T(8,128)}, f32[512,256]{1,0:T(8,128)}, f32[512,512]{0,1:T(8,128)}), (f32[512,256]{1,0:T(8,128)}, f32[512,256]{1,0:T(8,128)}, f32[512,512]{0,1:T(8,128)})) %all-reduce.9.cloned.1.call-update) | async-done | bytes 2097168 | tf_op jit(solution)/shard_map/psum | solution.py:9
  630.3 1.4 convert_add_fusion.1
  631.7 8.2 while.7
  639.9 39.3 %custom-call.6 = f32[4,128,128]{1,2,0:T(8,128)S(1)} custom-call(f32[4,128,128]{2,1,0:T(8,128)S(1)} %get-tuple-element.28), custom_call_target="InvertDiagBlocksLowerTriangular" | custom-call | tf_op jit(solution)/shard_map/triangular_solve/custom-call.1 | solution.py:13
  681.8 1.6 gather_fusion.3
  684.6 2.7 broadcast_select_fusion
  687.3 1.6 gather_fusion.4
  690.0 215.8 %all-reduce.7.cloned.1.call-done = (f32[512,256]{1,0:T(8,128)}, f32[512,256]{1,0:T(8,128)}, f32[512,512]{0,1:T(8,128)}) async-done(((f32[512,256]{1,0:T(8,128)}, f32[512,256]{1,0:T(8,128)}, f32[512,512]{0,1:T(8,128)}), (f32[512,256]{1,0:T(8,128)}, f32[512,256]{1,0:T(8,128)}, f32[512,512]{0,1:T(8,128)})) %all-reduce.7.cloned.1.call-update) | async-done | bytes 2097168 | tf_op jit(solution)/shard_map/psum | solution.py:9
  905.8 1.4 convert_add_fusion
  907.2 8.6 while.8
  910.1 1.4 dynamic-slice.21
  912.2 1.4 dynamic-slice.21
  915.8 39.5 %custom-call.7 = f32[4,128,128]{1,2,0:T(8,128)S(1)} custom-call(f32[4,128,128]{2,1,0:T(8,128)S(1)} %get-tuple-element.29), custom_call_target="InvertDiagBlocksLowerTriangular" | custom-call | tf_op jit(solution)/shard_map/triangular_solve/custom-call.1 | solution.py:13
  957.9 1.6 gather_fusion.5
  960.7 2.7 fusion.1
  (149 shorter events, 36.0 us)
Async XLA Ops:
  6.5 3.2 copy-start
  6.5 65.1 %all-gather.7.cloned.1.call-start = ((), (), s32[]{:S(2)}) async-start(), calls=%async_computation | async-start | bytes 1114112 | tf_op jit(solution)/shard_map/all_gather | solution.py:24
  8.2 123.7 %all-gather.9.cloned.1.call-start = ((), (), s32[]{:S(2)}) async-start(), calls=%async_computation.1 | async-start | bytes 1114112 | tf_op jit(solution)/shard_map/all_gather | solution.py:24
  9.0 0.7 copy-start.10
  9.0 342.8 %all-reduce.11.cloned.1.call-start = ((), (), s32[]{:S(2)}) async-start(), calls=%async_computation.5 | async-start | bytes 4194304 | tf_op jit(solution)/shard_map/psum | solution.py:9
  74.0 338.5 %all-gather.11.cloned.1.call-start = ((), (), s32[]{:S(2)}) async-start(), calls=%async_computation.2 | async-start | bytes 1114112 | tf_op jit(solution)/shard_map/all_gather | solution.py:24
  74.8 555.5 %all-reduce.9.cloned.1.call-start = ((), (), s32[]{:S(2)}) async-start(), calls=%async_computation.4 | async-start | bytes 4194304 | tf_op jit(solution)/shard_map/psum | solution.py:9
  353.3 48.2 %copy-start.4 = (f32[512,256]{1,0:T(8,128)S(1)}, f32[512,256]{1,0:T(8,128)}, u32[]{:S(2)}) copy-start(f32[512,256]{1,0:T(8,128)} %get-tuple-element.91) | copy-start | bytes 1572868
  404.0 1.6 copy-start.7
  405.6 1.2 copy-start.2
  412.1 493.7 %all-reduce.7.cloned.1.call-start = ((), (), s32[]{:S(2)}) async-start(), calls=%async_computation.3 | async-start | bytes 4194304 | tf_op jit(solution)/shard_map/psum | solution.py:9
  631.7 47.6 %copy-start.5 = (f32[512,256]{1,0:T(8,128)S(1)}, f32[512,256]{1,0:T(8,128)}, u32[]{:S(2)}) copy-start(f32[512,256]{1,0:T(8,128)} %get-tuple-element.88) | copy-start | bytes 1572868
  681.8 1.6 copy-start.8
  683.4 1.2 copy-start.1
  907.2 48.2 %copy-start.6 = (f32[512,256]{1,0:T(8,128)S(1)}, f32[512,256]{1,0:T(8,128)}, u32[]{:S(2)}) copy-start(f32[512,256]{1,0:T(8,128)} %get-tuple-element.85) | copy-start | bytes 1572868
  957.9 1.6 copy-start.9
  959.5 1.2 copy-start.3
Sparse Core Ops, SparseCore 0:
  10.3 61.2 all-gather.6
  74.7 57.2 all-gather.8
  134.5 217.3 all-reduce.10
  354.7 56.0 all-gather.10
  413.2 217.0 all-reduce.8
  690.0 215.7 all-reduce.6
where the time goes:
time: 971 us; the launch traced here: 970 us
  waiting for transfers between devices  765 us (79%)
  other arithmetic  133 us (14%)
  local copies, waits for them, and re-layouts  39.9 us (4%)
  matrix products  17.5 us (2%)
  between operations  14.1 us (1%)
    psum x3, waiting for transfers between devices, spread(): return lax.psum(block, axis)  649 us
    another operation x11, other arithmetic, forward_solve(): lax.linalg.triangular_solve(unit_lower, rhs, left_side=True, lower=True,...  122 us
    all_gather x3, waiting for transfers between devices, local(): panel = lax.all_gather(panels[tick], 'col', axis=1, tiled=True)  116 us
    another operation x64, local copies, waits for them, and re-layouts, forward_solve(): lax.linalg.triangular_solve(unit_lower, rhs, left_side=True, lower=True,...  25.2 us
  transfers between devices with their start and end apart: 6, of which 5 were waited for; matrix products, arithmetic and copies ran while one was open for 7% of the time, Pallas kernels for 0%

commit v1 on v0

v1 whole, which is shorter than its diff:
```python
import functools

import jax
import jax.numpy as jnp
from jax import lax
from jax.experimental import pallas as pl
from jax.experimental.pallas import tpu as pltpu
from jax.sharding import PartitionSpec as P

MESH = pl.DeviceIdType.MESH
HIGHEST = lax.Precision.HIGHEST
SIDE = 4
SLOTS = 64
CHUNKS = 16
LAG = 2
TILE = 128


def contract(a, b):
    return lax.dot_general(
        a, b, (((0,), (0,)), ((), ())), precision=HIGHEST, preferred_element_type=jnp.float32
    )


def exchange_kernel(tops, z_size, top_ref, piece_ref, x_ref, g_ref, xo_ref, *sems):
    (zp_s, zp_r, zm_s, zm_r, pr_s, pr_r, b_r, bp_s, bm_s, bc_s, x_s, x_r, loc) = sems
    row, col = lax.axis_index("row"), lax.axis_index("col")
    z, core = row // 2, row % 2
    xx, yy = col // SIDE, col % SIDE
    up = (2 * ((z + 1) % z_size) + core, col)
    down = (2 * ((z + z_size - 1) % z_size) + core, col)
    partner = (2 * z + 1 - core, col)

    def side(step_x, step_y):
        return (row, ((xx + step_x) % SIDE) * SIDE + (yy + step_y) % SIDE)

    barrier = pltpu.get_barrier_semaphore()
    near = (up, down, partner, side(1, 0), side(SIDE - 1, 0), side(0, 1), side(0, SIDE - 1))
    for device in near:
        pl.semaphore_signal(barrier, inc=1, device_id=device, device_id_type=MESH)
    pl.semaphore_wait(barrier, len(near))

    count, height = piece_ref.shape[0], top_ref.shape[0]
    base = tops * height
    chunk = height // CHUNKS

    def remote(src, dst, send, recv, device):
        return pltpu.make_async_remote_copy(
            src_ref=src, dst_ref=dst, send_sem=send, recv_sem=recv, device_id=device, device_id_type=MESH
        )

    def slot(origin_z):
        return g_ref.at[pl.ds(pl.multiple_of(base + (2 * origin_z + core) * count, 8), count), :]

    my_piece = pltpu.make_async_copy(piece_ref, slot(z), loc.at[0])
    my_x = pltpu.make_async_copy(x_ref, xo_ref.at[col], loc.at[1])
    my_piece.start()
    my_x.start()

    ups, downs = z_size // 2, z_size - 1 - z_size // 2

    def send_up(s):
        ref = slot((z + z_size - s) % z_size)
        return remote(ref, ref, zp_s.at[s], zp_r.at[s], up)

    def send_down(s):
        ref = slot((z + s) % z_size)
        return remote(ref, ref, zm_s.at[s], zm_r.at[s], down)

    def got_up(s):
        ref = slot((z + 2 * z_size - 1 - s) % z_size)
        return remote(ref, ref, zp_s.at[s], zp_r.at[s], up)

    def got_down(s):
        ref = slot((z + 1 + s) % z_size)
        return remote(ref, ref, zm_s.at[s], zm_r.at[s], down)

    def share(hops):
        ref = slot((z + z_size - hops) % z_size)
        return remote(ref, ref, pr_s.at[hops], pr_r.at[hops], partner)

    def ring_step(s):
        @pl.when(s <= ups)
        def _():
            got_up(s - 1).wait_recv()

            @pl.when(s < ups)
            def _():
                send_up(s).start()

            share(s).start()

        @pl.when(s <= downs)
        def _():
            got_down(s - 1).wait_recv()

            @pl.when(s < downs)
            def _():
                send_down(s).start()

            share(z_size - s).start()

    def top_rows(b, i):
        return g_ref.at[pl.ds(pl.multiple_of(b * height + i * chunk, 8), chunk), :]

    def hops_of(b):
        h = (z + z_size - b // 2) % z_size
        return h, jnp.where(h <= ups, h, z_size - h)

    def top_copy(b, i, kind):
        ref = top_rows(b, i)
        send, device = {"up": (bp_s, up), "down": (bm_s, down), "core": (bc_s, partner)}[kind]
        return remote(ref, ref, send.at[b, i], b_r.at[b, i], device)

    def top_roles(b):
        h, hops = hops_of(b)
        mine = core == b % 2
        return mine, mine & (h < ups), mine & ((h == 0) | (h > ups + 1)), mine & (h > 0), hops

    def top_step(t):
        for b in range(tops):
            mine, to_up, to_down, gets, hops = top_roles(b)
            i = t - LAG * hops
            inside = (i >= 0) & (i < CHUNKS)

            @pl.when(inside & gets)
            def _():
                top_copy(b, i, "up").wait_recv()

            @pl.when(inside & to_up)
            def _():
                top_copy(b, i, "up").start()

            @pl.when(inside & to_down)
            def _():
                top_copy(b, i, "down").start()

            @pl.when(inside & mine)
            def _():
                top_copy(b, i, "core").start()

    rows = x_ref.shape[0]
    half, quarter = rows // 2, rows // 4

    def x_piece(k, first, second, part):
        a = (xx if k == 0 else yy) + first
        b = (yy if k == 0 else xx) + second
        a, b = a % SIDE, b % SIDE
        c = a * SIDE + b if k == 0 else b * SIDE + a
        start, size = {"all": (0, half), "low": (0, quarter), "high": (quarter, quarter)}[part]
        return xo_ref.at[c, pl.ds(k * half + start, size), :]

    def x_send(k, stage, v, e, receive=False):
        first = (0, SIDE - 1, 1, 2)[v]
        move = {0: (0, "all"), 1: (0, "all"), 2: (SIDE - 1, "low"), 3: (1, "high")}[e]
        step = 1 if e in (0, 2) else SIDE - 1
        along_x = (k == 0) == (stage == 0)
        device = side(step, 0) if along_x else side(0, step)
        n = (k * 5 + (0 if stage == 0 else 1 + v)) * 4 + e
        back = {0: (SIDE - 1, "all"), 1: (1, "all"), 2: (2, "low"), 3: (2, "high")}[e]
        if stage == 0:
            src, dst = x_piece(k, move[0], 0, move[1]), x_piece(k, back[0], 0, back[1])
        else:
            src, dst = x_piece(k, first, move[0], move[1]), x_piece(k, first, back[0], back[1])
        if e < 2 and (stage == 0 or v == 0):
            src_send = x_ref.at[pl.ds(k * half, half), :]
        else:
            src_send = src
        if receive:
            return remote(dst, dst, x_s.at[n], x_r.at[n], device)
        return remote(src_send, src, x_s.at[n], x_r.at[n], device)

    def start(stage, v, e):
        for k in range(2):
            x_send(k, stage, v, e).start()

    def arrive(stage, v, e):
        for k in range(2):
            x_send(k, stage, v, e, True).wait_recv()

    def pair(stage, v, fns):
        for e in fns:
            start(stage, v, e)

    def pass_on(stage, v):
        arrive(stage, v, 0)
        start(stage, v, 2)
        arrive(stage, v, 1)
        start(stage, v, 3)

    def x_event(number):
        if number == 0:
            arrive(0, 0, 0)
            start(0, 0, 2)
            pair(1, 1, (0, 1))
            arrive(0, 0, 1)
            start(0, 0, 3)
            pair(1, 2, (0, 1))
        elif number == 1:
            pass_on(1, 0)
        elif number == 2:
            arrive(0, 0, 2)
            arrive(0, 0, 3)
            pair(1, 3, (0, 1))
        elif number == 3:
            pass_on(1, 1)
        elif number == 4:
            pass_on(1, 2)
        elif number == 5:
            pass_on(1, 3)

    pair(0, 0, (0, 1))
    pair(1, 0, (0, 1))
    my_piece.wait()
    send_up(0).start()
    send_down(0).start()
    share(0).start()
    if tops:
        for b in range(tops):
            @pl.when(row == b)
            def _():
                own = pltpu.make_async_copy(top_ref, g_ref.at[pl.ds(b * height, height), :], loc.at[2])
                own.start()
                own.wait()
    my_x.wait()

    total = LAG * ups + (CHUNKS if tops else 1)
    marks = [2 + (total - 2) * m // 6 for m in range(6)] + [total]
    begin = 0
    for number, end in enumerate(marks):
        def step(t, carry):
            if tops:
                top_step(t)
            s = t // LAG

            @pl.when((t % LAG == 0) & (s >= 1))
            def _():
                ring_step(s)

            return carry

        lax.fori_loop(begin, end, step, 0)
        begin = end
        x_event(number)

    for v in range(4):
        arrive(1, v, 2)
        arrive(1, v, 3)

    def drain_up(s, carry):
        send_up(s).wait_send()
        return carry

    def drain_down(s, carry):
        send_down(s).wait_send()
        return carry

    def drain_share(s, carry):
        share(s).wait_send()
        ref = slot((z + z_size - s) % z_size)
        other = g_ref.at[pl.ds(pl.multiple_of(base + (2 * ((z + z_size - s) % z_size) + 1 - core) * count, 8), count), :]
        remote(ref, other, pr_s.at[s], pr_r.at[s], partner).wait_recv()
        return carry

    lax.fori_loop(0, ups, drain_up, 0)
    lax.fori_loop(0, downs, drain_down, 0)
    lax.fori_loop(0, z_size, drain_share, 0)
    if tops:
        def drain_top(i, carry):
            for b in range(tops):
                mine, to_up, to_down, gets, hops = top_roles(b)

                @pl.when(jnp.logical_not(mine))
                def _():
                    top_copy(b, i, "core").wait_recv()

                @pl.when(to_up)
                def _():
                    top_copy(b, i, "up").wait_send()

                @pl.when(to_down)
                def _():
                    top_copy(b, i, "down").wait_send()

                @pl.when(mine)
                def _():
                    top_copy(b, i, "core").wait_send()

            return carry

        lax.fori_loop(0, CHUNKS, drain_top, 0)
    for k in range(2):
        for e in range(4):
            x_send(k, 0, 0, e).wait_send()
        for v in range(4):
            for e in range(4):
                x_send(k, 1, v, e).wait_send()


def exchange(top, piece, x, tops, owners, ident):
    height, width = top.shape
    count = piece.shape[0]
    z_size = owners // 2
    dma = pltpu.SemaphoreType.DMA
    vmem = pl.BlockSpec(memory_space=pltpu.VMEM)
    hbm = pl.BlockSpec(memory_space=pl.ANY)
    blocks = max(tops, 1)
    g, xo = pl.pallas_call(
        functools.partial(exchange_kernel, tops, z_size),
        out_shape=(
            jax.ShapeDtypeStruct((tops * height + owners * count, width), jnp.float32),
            jax.ShapeDtypeStruct((SIDE * SIDE,) + x.shape, jnp.float32),
        ),
        in_specs=[vmem, vmem, vmem],
        out_specs=(hbm, hbm),
        scratch_shapes=[
            dma((z_size,)), dma((z_size,)), dma((z_size,)), dma((z_size,)),
            dma((z_size,)), dma((z_size,)),
            dma((blocks, CHUNKS)), dma((blocks, CHUNKS)), dma((blocks, CHUNKS)), dma((blocks, CHUNKS)),
            dma((40,)), dma((40,)), dma((3,)),
        ],
        compiler_params=pltpu.CompilerParams(collective_id=ident, has_side_effects=True),
    )(top, piece, x)
    return g, xo.reshape(SIDE * SIDE * x.shape[0], x.shape[1])


def invert_tile(tile):
    k = lax.broadcasted_iota(jnp.int32, tile.shape, 0)
    r = lax.broadcasted_iota(jnp.int32, tile.shape, 1)
    mul = functools.partial(jnp.dot, precision=HIGHEST, preferred_element_type=jnp.float32)
    eye = jnp.where(k == r, 1.0, 0.0).astype(jnp.float32)
    strict = jnp.where(k < r, tile, 0.0)
    power = jnp.where(k // 16 == r // 16, -strict, 0.0)
    inverse = eye + power
    for _ in range(3):
        power = mul(power, power)
        inverse = inverse + mul(inverse, power)
    for size in (16, 32, 64):
        off = jnp.where((k // (2 * size) == r // (2 * size)) & (k // size != r // size), strict, 0.0)
        inverse = inverse - mul(inverse, mul(off, inverse))
    return inverse


def solve_kernel(ticks, width, x_ref, t_ref, u_ref, inverse_ref):
    tiles = width // TILE

    def invert(n, carry):
        b, j = n // tiles, n % tiles
        across = pl.ds(pl.multiple_of(n * TILE, TILE), TILE)
        inverse_ref[across, :] = invert_tile(x_ref[pl.ds(pl.multiple_of(j * TILE, TILE), TILE), across])
        return carry

    lax.fori_loop(0, ticks * tiles, invert, 0)
    off = ticks * width
    for b in range(ticks):
        rhs = t_ref[pl.ds(b * width, width), :]
        for j in range(b):
            block = x_ref[:, pl.ds(off, width)]
            off += width
            rhs = rhs - contract(block, u_ref[pl.ds(j * width, width), :])
        for j in range(tiles):
            here = b * width + j * TILE
            part = rhs[j * TILE:(j + 1) * TILE]
            if j:
                part = part - contract(
                    x_ref[pl.ds(0, j * TILE), pl.ds(here, TILE)], u_ref[pl.ds(b * width, j * TILE), :]
                )
            u_ref[pl.ds(here, TILE), :] = contract(inverse_ref[pl.ds(here, TILE), :], part)


def solve(x, t, ticks, width):
    vmem = pl.BlockSpec(memory_space=pltpu.VMEM)
    return pl.pallas_call(
        functools.partial(solve_kernel, ticks, width),
        out_shape=jax.ShapeDtypeStruct(t.shape, jnp.float32),
        in_specs=[vmem, vmem],
        out_specs=vmem,
        scratch_shapes=[pltpu.VMEM((ticks * width, TILE), jnp.float32)],
        compiler_params=pltpu.CompilerParams(vmem_limit_bytes=50 * 1024 * 1024),
    )(x, t)


def find(a, b, base):
    i = jnp.arange(b.shape[0], dtype=jnp.int32)
    return jnp.max(jnp.where(a[:, None] == b[None, :], base + i[None, :], -1), axis=1)


def packing(pivots, rows):
    src = pivots.reshape(-1)
    owner = src // rows
    e = jnp.arange(src.shape[0], dtype=jnp.int32)
    same = (owner[:, None] == owner[None, :]) & (e[None, :] < e[:, None])
    return src, owner, jnp.sum(same.astype(jnp.int32), axis=1)


def update(packed, owners, slab, panels, pivots):
    rows, cols = slab.shape
    ticks, width = pivots.shape
    depth = panels.shape[2]
    me = lax.axis_index("row")
    src, owner, rank = packing(pivots, rows)
    top = ticks * width
    ident = 0 if packed else 2
    panel_rows = jnp.concatenate(
        [panels[k] for k in range(ticks)] + [jnp.zeros((rows, 128 - ticks * depth), jnp.float32)], axis=1
    )
    if packed:
        count, tops, patch = SLOTS, ticks, 128
        g = jnp.where(owner < ticks, src, top + owner * count + rank)
        s = jnp.arange(count, dtype=jnp.int32)
        held = (owner[None, :] == me) & (rank[None, :] == s[:, None])
        listed = jnp.max(jnp.where(held, src[None, :] - me * rows, 0), axis=1)
        panel_piece = jnp.take(panel_rows, listed, axis=0)
        slab_piece = jnp.take(slab, listed, axis=0)
    else:
        count, tops, patch = rows, 0, rows
        g = src
        panel_piece, slab_piece = panel_rows, slab

    x_panels = jnp.transpose(panels, (2, 0, 1)).reshape(depth, ticks * rows)
    g_panel, full = exchange(panel_rows, panel_piece, x_panels, tops, owners, ident)

    s0, s1, s2 = pivots
    g0, g1, g2 = g[:width], g[width:2 * width], g[2 * width:]
    back = find(s2, s1, width)
    f2 = find(jnp.where(back >= 0, back, s2), s0, 0)
    f1 = find(s1, s0, 0)
    row20 = jnp.where(back >= 0, back, g2)
    take_t = jnp.concatenate([g0, jnp.where(f1 >= 0, f1, g1), jnp.where(f2 >= 0, f2, row20)])
    mine = me * rows + jnp.arange(rows, dtype=jnp.int32)
    h2 = find(mine, s2, 2 * width)
    pos1 = jnp.where(h2 >= 0, h2, mine)
    h1 = find(pos1, s1, width)
    pos0 = jnp.where(h1 >= 0, h1, pos1)
    h0 = find(pos0, s0, 0)
    orig = jnp.where(h0 >= 0, h0, pos0)
    moved0, moved1 = pos0 != mine, pos1 != mine
    if packed:
        touched = orig != mine
        q = jnp.arange(rows, dtype=jnp.int32)
        place = jnp.sum(((q[None, :] < q[:, None]) & touched[None, :]).astype(jnp.int32), axis=1)
        s = jnp.arange(patch, dtype=jnp.int32)
        pick = (place[None, :] == s[:, None]) & touched[None, :]
        from0 = jnp.max(jnp.where(pick & moved0[None, :], pos0[None, :], 0), axis=1)
        from1 = jnp.max(jnp.where(pick & moved1[None, :], pos1[None, :], 0), axis=1)
    else:
        from0, from1 = pos0, pos1
    corner = jnp.concatenate([
        g_panel[:width, 0:depth],
        g_panel[width:2 * width, depth:2 * depth],
        g_panel[2 * width:3 * width, 2 * depth:3 * depth],
        jnp.take(g_panel, g1, axis=0)[:, 0:depth],
        jnp.take(g_panel, row20, axis=0)[:, 0:depth],
        jnp.take(g_panel, g2, axis=0)[:, depth:2 * depth],
        jnp.take(g_panel, from0, axis=0)[:, 0:depth],
        jnp.take(g_panel, from1, axis=0)[:, depth:2 * depth],
    ]).T
    g_slab, factor = exchange(slab, slab_piece, corner, tops, owners, ident + 1)

    t = jnp.take(g_slab, take_t, axis=0)
    kept = jnp.take(g_slab, jnp.where(orig != mine, orig, 0), axis=0)
    base = jnp.where((orig != mine)[:, None], kept, slab)
    left = []
    for k, moved in ((0, moved0), (1, moved1)):
        new = factor[:, 2 * top + k * patch:2 * top + (k + 1) * patch]
        if packed:
            new = jnp.dot(new, pick.astype(jnp.float32), precision=HIGHEST, preferred_element_type=jnp.float32)
        left.append(jnp.where(moved[None, :], new, full[:, k * rows:(k + 1) * rows]))
    left.append(full[:, 2 * rows:3 * rows])
    return factor[:, :2 * top + 2 * 128], t, base, left


def solution(mesh):
    owners = mesh.shape["row"]

    def local(slab, panels, pivots):
        rows, ticks = slab.shape[0], pivots.shape[0]
        _, owner, rank = packing(pivots, rows)
        fits = jnp.all((owner < ticks) | (rank < SLOTS))
        factor, t, base, left = lax.cond(
            fits,
            functools.partial(update, True, owners),
            functools.partial(update, False, owners),
            slab, panels, pivots,
        )
        width = pivots.shape[1]
        upper = solve(factor, t, ticks, width)
        me = lax.axis_index("row")
        lowered = base
        for k in range(ticks):
            lowered = lowered - contract(left[k], upper[k * width:(k + 1) * width])
        for k in range(ticks):
            lowered = jnp.where(me == k, upper[k * width:(k + 1) * width], lowered)
        return lowered

    in_specs = (P("row", "col"), P(None, "row", "col"), P())
    return jax.shard_map(local, mesh=mesh, in_specs=in_specs, out_specs=P("row", "col"), check_vma=False)
```

time: 971 us -> 238 us (0.25)
  the two profiles are of different devices: /device:TPU:1 before, /device:TPU:257 now
where the time goes in v1:
time: 238 us; the launch traced here: 234 us
  Pallas kernels  170 us (71%)
  local copies, waits for them, and re-layouts  27.7 us (12%)
  matrix products  13.2 us (6%)
  other arithmetic  12.1 us (5%)
  loops' own time  10.5 us (4%)
    pallas_call x2, Pallas kernels, exchange(): pl.pallas_call(functools.partial(exchange_kernel, tops, z_size), out_shap...  129 us
    pallas_call x1, Pallas kernels, solve(): pl.pallas_call(functools.partial(solve_kernel, ticks, width), out_shape=j...  40.6 us
    another operation x1, loops' own time, local(): lax.cond(fits, functools.partial(update, True, owners), functools.partial...  10.5 us
    dot_general x3, matrix products, contract(): lax.dot_general(a, b, (((0,), (0,)), ((), ())), precision=HIGHEST, prefer...  8.39 us
    gather x1, local copies, waits for them, and re-layouts, update(): t = jnp.take(g_slab, take_t, axis=0)  5.7 us
    reduce_sum x2, other arithmetic, packing(): return (src, owner, jnp.sum(same.astype(jnp.int32), axis=1))  5.34 us
    dot_general x2, matrix products, update(): jnp.dot(new, pick.astype(jnp.float32), precision=HIGHEST, preferred_eleme...  4.8 us

profile of v1, /device:TPU:257, one launch (start us, length us, event | category | flops | bytes accessed | tf_op | source)
XLA Modules:
  0.0 234.4 jit_solution(18232326347387198631)
XLA Ops:
  0.0 0.7 reshape.719
  0.7 2.7 %convert_reduce_fusion.2 = s32[1536]{0:T(1024)S(1)} fusion(s32[1536]{0:T(1024)S(1)} %add_select_fusion.2), kind=kLoop, calls=%fused_computation.180 | loop fusion | flops 11794944 | bytes 12288 | tf_op jit(solution)/shard_map/reduce_sum | solution.py:393
  3.4 1.4 or_reduce_fusion
  5.4 178.9 %conditional.1 = (f32[512,3328]{1,0:T(8,128)}, f32[1536,256]{1,0:T(8,128)}, f32[512,256]{1,0:T(8,128)S(1)}, f32[512,512]{1,0:T(8,128)}, f32[512,512]{1,0:T(8,128)S(1)}, /*index=5*/f32[512,512]{1,0:T(8,128)}) conditional(s32[]{:T(128)} %convert_element_type.15, (f32[3,512,32]{1,2,0:T(8,128)}, s32[3,512]{1,0:T(4,128)}, ...), branch_computations={%region_2.10_spmd, %region_9.24_spmd} | conditional | flops 825649152 | bytes 92687840 | solution.py:480
  5.7 0.7 reshape.714
  6.5 2.7 %convert_reduce_fusion = s32[1536]{0:T(1024)S(1)} fusion(s32[1536]{0:T(1024)S(1)} %add_select_fusion), kind=kLoop, calls=%fused_computation.79 | loop fusion | flops 11794944 | bytes 12288 | tf_op jit(solution)/shard_map/cond/branch_1_fun/reduce_sum | solution.py:393
  9.4 1.2 copy.63
  11.6 0.7 broadcast_select_fusion.3.piece_ref
  12.3 0.7 copy.77
  13.0 63.1 %branch_1_fun.2 = (f32[3584,128]{1,0:T(8,128)}, f32[16,32,1536]{2,1,0:T(8,128)}) custom-call(f32[512,128]{1,0:T(8,128)} %copy-done.7, f32[64,128]{1,0:T(8,128)} %broadcast_select_fusion.3.piece_ref, f32[32,1536]{1,0:T(8,128)} %bitcast.76), custom_call_target="tpu_custom_call" | custom-call | tf_op jit(solution)/shard_map/cond/branch_1_fun/pallas_call | solution.py:308
  76.1 2.9 %copy.54 = f32[3584,128]{0,1:T(8,128)} copy(f32[3584,128]{1,0:T(8,128)} %get-tuple-element.30) | data formatting | bytes 3670016 | tf_op jit(solution)/shard_map/cond/branch_1_fun/pallas_call | solution.py:308
  79.0 0.8 slice_dynamic-update-slice_fusion.5
  79.8 0.8 slice_dynamic-update-slice_fusion.4
  80.7 0.8 slice_dynamic-update-slice_fusion.3
  83.0 1.0 gather_fusion.11
  84.2 1.0 gather_fusion.12
  85.8 1.0 gather_fusion.13
  87.1 0.6 gather_fusion.14
  88.7 0.7 gather_fusion.7
  89.3 0.7 broadcast_select_fusion.2.piece_ref
  90.0 66.2 %branch_1_fun.3 = (f32[3584,256]{1,0:T(8,128)}, f32[16,32,3328]{2,1,0:T(8,128)}) custom-call(f32[512,256]{1,0:T(8,128)S(1)} %copy-done.2, f32[64,256]{1,0:T(8,128)} %broadcast_select_fusion.2.piece_ref, f32[32,3328]{1,0:T(8,128)} %bitcast.79), custom_call_target="tpu_custom_call" | custom-call | tf_op jit(solution)/shard_map/cond/branch_1_fun/pallas_call | solution.py:308
  156.3 1.9 convolution_select_fusion
  158.2 2.9 %convolution_select_fusion.1 = f32[512,512]{1,0:T(8,128)} fusion(f32[512,1536]{1,0:T(8,128)} %bitcast.66, pred[512]{0:T(512)(128)(4,1)S(1)} %get-tuple-element.82, f32[512,3328]{1,0:T(8,128)} %bitcast.61, s32[512]{0:T(512)S(1)} %convert_reduce_fusion.1, pred[512]{0:T(512)(128)(4,1)S(1)} %get-tuple-element.127), kind=kOutput, calls=%fused_computation.83 | convolution fusion | flops 403046400 | bytes 2362368 | tf_op jit(solution)/shard_map/cond/branch_1_fun/dot_general | solution.py:467
  161.1 5.7 %gather_fusion.9 = f32[1536,256]{1,0:T(8,128)S(1)} fusion(f32[3584,256]{1,0:T(8,128)} %get-tuple-element.32, s32[2048]{0:T(1024)S(1)} %pad_clamp_fusion.7), kind=kCustom, calls=%fused_computation.14 | custom fusion | bytes 3151872 | tf_op jit(solution)/shard_map/cond/branch_1_fun/jit(_take)/gather | solution.py:460
  166.9 1.4 broadcast_select_fusion.1
  168.3 3.6 %gather_fusion.10 = f32[512,256]{1,0:T(8,128)S(1)} fusion(f32[3584,256]{1,0:T(8,128)} %get-tuple-element.32, s32[1024]{0:T(1024)S(1)} %get-tuple-element.128), kind=kCustom, calls=%fused_computation.15 | custom fusion | bytes 1050624 | tf_op jit(solution)/shard_map/cond/branch_1_fun/jit(_take)/gather | solution.py:461
  172.1 2.3 slice.202
  184.3 0.8 copy-done.8
  185.1 40.6 %shard_map.37 = f32[1536,256]{1,0:T(8,128)S(1)} custom-call(f32[512,3328]{1,0:T(8,128)} %get-tuple-element.40.x_ref, f32[1536,256]{1,0:T(8,128)} %get-tuple-element.41.t_ref), custom_call_target="tpu_custom_call" | custom-call | tf_op jit(solution)/shard_map/pallas_call | solution.py:373
  225.8 1.8 convolution_subtract_fusion.2
  227.6 2.6 %convolution_subtract_fusion.1 = f32[512,256]{1,0:T(8,128)} fusion(f32[512,256]{1,0:T(8,128)S(1)} %convolution_subtract_fusion.2, f32[512,512]{1,0:T(8,128)S(1)} %get-tuple-element.44, f32[1536,256]{1,0:T(8,128)S(1)} %shard_map.37), kind=kOutput, calls=%fused_computation.184 | convolution fusion | flops 805437440 | bytes 2621440 | tf_op jit(solution)/shard_map/dot_general | solution.py:20
  230.2 4.0 %fusion.28 = f32[512,256]{1,0:T(8,128)} fusion(f32[512,256]{1,0:T(8,128)} %convolution_subtract_fusion.1, f32[512,512]{1,0:T(8,128)} %get-tuple-element.45, f32[1536,256]{1,0:T(8,128)S(1)} %shard_map.37, pred[]{:T(512)S(6)} %eq.154, pred[]{:T(512)S(6)} %eq.153, pred[]{:T(512)S(6)} %eq.149), kind=kOutput, calls=%fused_computation.188 | convolution fusion | flops 805830656 | bytes 4194307 | tf_op jit(solution)/shard_map/dot_general | solution.py:20
  (71 shorter events, 4.7 us)
Async XLA Ops:
  5.7 6.6 %copy-start.6 = (f32[3,512,32]{1,2,0:T(8,128)S(1)}, f32[3,512,32]{1,2,0:T(8,128)}, u32[]{:S(2)}) copy-start(f32[3,512,32]{1,2,0:T(8,128)} %get-tuple-element.63) | copy-start | bytes 589828 | tf_op jit(solution)/shard_map/cond
  10.8 70.8 %copy-start.12 = (s32[3,512]{1,0:T(4,128)S(1)}, s32[3,512]{1,0:T(4,128)}, u32[]{:S(2)}) copy-start(s32[3,512]{1,0:T(4,128)} %get-tuple-element.28) | copy-start | bytes 18436 | tf_op jit(solution)/shard_map/cond
  11.0 2.0 copy-start.7
  76.1 6.9 %copy-start = (f32[3584,128]{1,0:T(8,128)S(1)}, f32[3584,128]{1,0:T(8,128)}, u32[]{:S(2)}) copy-start(f32[3584,128]{1,0:T(8,128)} %get-tuple-element.30) | copy-start | bytes 5505028 | tf_op jit(solution)/shard_map/cond
  85.2 3.4 %copy-start.2 = (f32[512,256]{1,0:T(8,128)S(1)}, f32[512,256]{1,0:T(8,128)}, u32[]{:S(2)}) copy-start(f32[512,256]{1,0:T(8,128)} %get-tuple-element.27.top_ref) | copy-start | bytes 1572868 | tf_op jit(solution)/shard_map/cond
  88.6 1.4 copy-start.11
  184.3 0.8 copy-start.8
  185.1 40.7 %copy-start.4 = (f32[512,512]{1,0:T(8,128)S(1)}, f32[512,512]{1,0:T(8,128)}, u32[]{:S(2)}) copy-start(f32[512,512]{1,0:T(8,128)} %get-tuple-element.43) | copy-start | bytes 3145732
  185.1 40.7 %copy-start.9 = (f32[512,256]{1,0:T(8,128)S(1)}, f32[512,256]{1,0:T(8,128)}, u32[]{:S(2)}) copy-start(f32[512,256]{1,0:T(8,128)} %copy-done.8) | copy-start | bytes 1572868

commit v2 on v1

--- a/solution.py
+++ b/solution.py
@@ -8,21 +8,26 @@
 from jax.sharding import PartitionSpec as P
 
 MESH = pl.DeviceIdType.MESH
-HIGHEST = lax.Precision.HIGHEST
 SIDE = 4
 SLOTS = 64
-CHUNKS = 16
-LAG = 2
+CHUNKS = 8
+LAG = 4
 TILE = 128
-
-
-def contract(a, b):
-    return lax.dot_general(
-        a, b, (((0,), (0,)), ((), ())), precision=HIGHEST, preferred_element_type=jnp.float32
-    )
-
-
-def exchange_kernel(tops, z_size, top_ref, piece_ref, x_ref, g_ref, xo_ref, *sems):
+PATCH = 128
+
+
+def split(a):
+    high = a.astype(jnp.bfloat16)
+    return high, (a - high.astype(jnp.float32)).astype(jnp.bfloat16)
+
+
+def mul(a, b):
+    dot = functools.partial(jnp.dot, preferred_element_type=jnp.float32)
+    (ah, al), (bh, bl) = split(a), split(b)
+    return dot(ah, bh) + (dot(ah, bl) + dot(al, bh))
+
+
+def exchange_kernel(tops, z_size, LAG, CHUNKS, top_ref, piece_ref, x_ref, g_ref, xo_ref, *sems):
     (zp_s, zp_r, zm_s, zm_r, pr_s, pr_r, b_r, bp_s, bm_s, bc_s, x_s, x_r, loc) = sems
     row, col = lax.axis_index("row"), lax.axis_index("col")
     z, core = row // 2, row % 2
@@ -53,7 +58,7 @@
         return g_ref.at[pl.ds(pl.multiple_of(base + (2 * origin_z + core) * count, 8), count), :]
 
     my_piece = pltpu.make_async_copy(piece_ref, slot(z), loc.at[0])
-    my_x = pltpu.make_async_copy(x_ref, xo_ref.at[col], loc.at[1])
+    my_x = pltpu.make_async_copy(x_ref, xo_ref.at[:, col], loc.at[1])
     my_piece.start()
     my_x.start()
 
@@ -139,7 +144,7 @@
             def _():
                 top_copy(b, i, "core").start()
 
-    rows = x_ref.shape[0]
+    rows = x_ref.shape[1]
     half, quarter = rows // 2, rows // 4
 
     def x_piece(k, first, second, part):
@@ -148,7 +153,7 @@
         a, b = a % SIDE, b % SIDE
         c = a * SIDE + b if k == 0 else b * SIDE + a
         start, size = {"all": (0, half), "low": (0, quarter), "high": (quarter, quarter)}[part]
-        return xo_ref.at[c, pl.ds(k * half + start, size), :]
+        return xo_ref.at[:, c, pl.ds(k * half + start, size), :]
 
     def x_send(k, stage, v, e, receive=False):
         first = (0, SIDE - 1, 1, 2)[v]
@@ -163,7 +168,7 @@
         else:
             src, dst = x_piece(k, first, move[0], move[1]), x_piece(k, first, back[0], back[1])
         if e < 2 and (stage == 0 or v == 0):
-            src_send = x_ref.at[pl.ds(k * half, half), :]
+            src_send = x_ref.at[:, pl.ds(k * half, half), :]
         else:
             src_send = src
         if receive:
@@ -297,87 +302,130 @@
                 x_send(k, 1, v, e).wait_send()
 
 
-def exchange(top, piece, x, tops, owners, ident):
+def exchange(top, piece, x, tops, owners, ident, lag=LAG, chunks=CHUNKS, space=pl.ANY):
     height, width = top.shape
     count = piece.shape[0]
     z_size = owners // 2
     dma = pltpu.SemaphoreType.DMA
     vmem = pl.BlockSpec(memory_space=pltpu.VMEM)
-    hbm = pl.BlockSpec(memory_space=pl.ANY)
+    hbm = pl.BlockSpec(memory_space=space)
     blocks = max(tops, 1)
     g, xo = pl.pallas_call(
-        functools.partial(exchange_kernel, tops, z_size),
+        functools.partial(exchange_kernel, tops, z_size, lag, chunks),
         out_shape=(
             jax.ShapeDtypeStruct((tops * height + owners * count, width), jnp.float32),
-            jax.ShapeDtypeStruct((SIDE * SIDE,) + x.shape, jnp.float32),
+            jax.ShapeDtypeStruct((x.shape[0], SIDE * SIDE) + x.shape[1:], jnp.float32),
         ),
         in_specs=[vmem, vmem, vmem],
         out_specs=(hbm, hbm),
         scratch_shapes=[
             dma((z_size,)), dma((z_size,)), dma((z_size,)), dma((z_size,)),
             dma((z_size,)), dma((z_size,)),
-            dma((blocks, CHUNKS)), dma((blocks, CHUNKS)), dma((blocks, CHUNKS)), dma((blocks, CHUNKS)),
+            dma((blocks, chunks)), dma((blocks, chunks)), dma((blocks, chunks)), dma((blocks, chunks)),
             dma((40,)), dma((40,)), dma((3,)),
         ],
         compiler_params=pltpu.CompilerParams(collective_id=ident, has_side_effects=True),
     )(top, piece, x)
-    return g, xo.reshape(SIDE * SIDE * x.shape[0], x.shape[1])
-
-
-def invert_tile(tile):
-    k = lax.broadcasted_iota(jnp.int32, tile.shape, 0)
-    r = lax.broadcasted_iota(jnp.int32, tile.shape, 1)
-    mul = functools.partial(jnp.dot, precision=HIGHEST, preferred_element_type=jnp.float32)
+    return g, xo.reshape(x.shape[0], SIDE * SIDE * x.shape[1], x.shape[2])
+
+
+def invert_tiles(tiles):
+    k = lax.broadcasted_iota(jnp.int32, tiles[0].shape, 0)
+    r = lax.broadcasted_iota(jnp.int32, tiles[0].shape, 1)
     eye = jnp.where(k == r, 1.0, 0.0).astype(jnp.float32)
-    strict = jnp.where(k < r, tile, 0.0)
-    power = jnp.where(k // 16 == r // 16, -strict, 0.0)
-    inverse = eye + power
+    strict = [jnp.where(k < r, tile, 0.0) for tile in tiles]
+    power = [jnp.where(k // 16 == r // 16, -tile, 0.0) for tile in strict]
+    inverse = [eye + tile for tile in power]
     for _ in range(3):
-        power = mul(power, power)
-        inverse = inverse + mul(inverse, power)
+        power = [mul(tile, tile) for tile in power]
+        inverse = [one + mul(one, tile) for one, tile in zip(inverse, power)]
     for size in (16, 32, 64):
-        off = jnp.where((k // (2 * size) == r // (2 * size)) & (k // size != r // size), strict, 0.0)
-        inverse = inverse - mul(inverse, mul(off, inverse))
+        pick = (k // (2 * size) == r // (2 * size)) & (k // size != r // size)
+        half = [mul(jnp.where(pick, tile, 0.0), one) for tile, one in zip(strict, inverse)]
+        inverse = [one - mul(one, tile) for one, tile in zip(inverse, half)]
     return inverse
 
 
-def solve_kernel(ticks, width, x_ref, t_ref, u_ref, inverse_ref):
+def finish_kernel(ticks, f_ref, full_ref, t_ref, base_ref, touched_ref, ints_ref, place_ref, moved_ref,
+                  out_ref, inv_ref, u_ref):
+    width = f_ref.shape[1]
     tiles = width // TILE
-
-    def invert(n, carry):
-        b, j = n // tiles, n % tiles
-        across = pl.ds(pl.multiple_of(n * TILE, TILE), TILE)
-        inverse_ref[across, :] = invert_tile(x_ref[pl.ds(pl.multiple_of(j * TILE, TILE), TILE), across])
+    inv_ref[...] = jnp.zeros_like(inv_ref)
+
+    def invert(b, carry):
+        spots = [pl.ds(j * TILE, TILE) for j in range(tiles)]
+        for spot, one in zip(spots, invert_tiles([f_ref[b, spot, spot] for spot in spots])):
+            inv_ref[b, spot, spot] = one
         return carry
 
-    lax.fori_loop(0, ticks * tiles, invert, 0)
-    off = ticks * width
+    lax.fori_loop(0, ticks, invert, 0)
+    size = TILE
+    while size < width:
+        spots = [
+            (b, pl.ds(low, size), pl.ds(low + size, size))
+            for b in range(ticks) for low in range(0, width, 2 * size)
+        ]
+        half = [mul(f_ref[b, near, far], inv_ref[b, far, far]) for b, near, far in spots]
+        for (b, near, far), tile in zip(spots, half):
+            inv_ref[b, near, far] = -mul(inv_ref[b, near, near], tile)
+        size *= 2
+
+    off = ticks
     for b in range(ticks):
-        rhs = t_ref[pl.ds(b * width, width), :]
+        rhs = t_ref[pl.ds(b * width, width), :].T
         for j in range(b):
-            block = x_ref[:, pl.ds(off, width)]
-            off += width
-            rhs = rhs - contract(block, u_ref[pl.ds(j * width, width), :])
-        for j in range(tiles):
-            here = b * width + j * TILE
-            part = rhs[j * TILE:(j + 1) * TILE]
-            if j:
-                part = part - contract(
-                    x_ref[pl.ds(0, j * TILE), pl.ds(here, TILE)], u_ref[pl.ds(b * width, j * TILE), :]
-                )
-            u_ref[pl.ds(here, TILE), :] = contract(inverse_ref[pl.ds(here, TILE), :], part)
-
-
-def solve(x, t, ticks, width):
+            rhs = rhs - mul(u_ref[j], f_ref[off])
+            off += 1
+        u_ref[b] = mul(rhs, inv_ref[b])
+
+    me = ints_ref[PATCH]
+
+    @pl.when(me < ticks)
+    def _():
+        out_ref[...] = u_ref[jnp.minimum(me, ticks - 1)].T
+
+    @pl.when(me >= ticks)
+    def _():
+        out_ref[...] = base_ref[...]
+
+        def place_row(s, carry):
+            to = ints_ref[s]
+
+            @pl.when(to >= 0)
+            def _():
+                out_ref[pl.ds(to, 1), :] = touched_ref[pl.ds(s, 1), :]
+
+            return carry
+
+        lax.fori_loop(0, PATCH, place_row, 0)
+        s = lax.broadcasted_iota(jnp.int32, (PATCH, place_ref.shape[1]), 0)
+        pick = jnp.where(place_ref[0:1, :] == s, 1.0, 0.0).astype(jnp.bfloat16)
+        total = None
+        for k in range(ticks):
+            left = full_ref[k]
+            if k < ticks - 1:
+                high, low = split(f_ref[off, :, pl.ds(k * PATCH, PATCH)])
+                new = jnp.dot(high, pick, preferred_element_type=jnp.float32)
+                new = new + jnp.dot(low, pick, preferred_element_type=jnp.float32)
+                left = jnp.where(moved_ref[k:k + 1, :] > 0, new, left)
+            part = mul(u_ref[k], left)
+            total = part if total is None else total + part
+        out_ref[...] = out_ref[...] - total.T
+
+
+def finish(ticks, factor, full, t, base, touched, ints, place, moved):
     vmem = pl.BlockSpec(memory_space=pltpu.VMEM)
+    width, cols = factor.shape[1], t.shape[1]
     return pl.pallas_call(
-        functools.partial(solve_kernel, ticks, width),
-        out_shape=jax.ShapeDtypeStruct(t.shape, jnp.float32),
-        in_specs=[vmem, vmem],
+        functools.partial(finish_kernel, ticks),
+        out_shape=jax.ShapeDtypeStruct(base.shape, jnp.float32),
+        in_specs=[vmem] * 5 + [pl.BlockSpec(memory_space=pltpu.SMEM), vmem, vmem],
         out_specs=vmem,
-        scratch_shapes=[pltpu.VMEM((ticks * width, TILE), jnp.float32)],
+        scratch_shapes=[
+            pltpu.VMEM((ticks, width, width), jnp.float32), pltpu.VMEM((ticks, cols, width), jnp.float32)
+        ],
         compiler_params=pltpu.CompilerParams(vmem_limit_bytes=50 * 1024 * 1024),
-    )(x, t)
+    )(factor, full, t, base, touched, ints, place, moved)
 
 
 def find(a, b, base):
@@ -393,32 +441,34 @@
     return src, owner, jnp.sum(same.astype(jnp.int32), axis=1)
 
 
-def update(packed, owners, slab, panels, pivots):
+def rows_of(array, index):
+    return jnp.take(array, index, axis=0, mode="clip")
+
+
+def update(packed, owners, slab, panels, pivots, packs):
     rows, cols = slab.shape
     ticks, width = pivots.shape
     depth = panels.shape[2]
     me = lax.axis_index("row")
-    src, owner, rank = packing(pivots, rows)
+    src, owner, rank = packs
     top = ticks * width
     ident = 0 if packed else 2
     panel_rows = jnp.concatenate(
         [panels[k] for k in range(ticks)] + [jnp.zeros((rows, 128 - ticks * depth), jnp.float32)], axis=1
     )
     if packed:
-        count, tops, patch = SLOTS, ticks, 128
+        count, tops, space = SLOTS, ticks, pltpu.VMEM
         g = jnp.where(owner < ticks, src, top + owner * count + rank)
         s = jnp.arange(count, dtype=jnp.int32)
         held = (owner[None, :] == me) & (rank[None, :] == s[:, None])
         listed = jnp.max(jnp.where(held, src[None, :] - me * rows, 0), axis=1)
-        panel_piece = jnp.take(panel_rows, listed, axis=0)
-        slab_piece = jnp.take(slab, listed, axis=0)
+        panel_piece, slab_piece = rows_of(panel_rows, listed), rows_of(slab, listed)
     else:
-        count, tops, patch = rows, 0, rows
+        count, tops, space = rows, 0, pl.ANY
         g = src
         panel_piece, slab_piece = panel_rows, slab
-
-    x_panels = jnp.transpose(panels, (2, 0, 1)).reshape(depth, ticks * rows)
-    g_panel, full = exchange(panel_rows, panel_piece, x_panels, tops, owners, ident)
+    x_panels = jnp.transpose(panels, (0, 2, 1))
+    g_panel, full = exchange(panel_rows, panel_piece, x_panels, tops, owners, ident, LAG, CHUNKS, space)
 
     s0, s1, s2 = pivots
     g0, g1, g2 = g[:width], g[width:2 * width], g[2 * width:]
@@ -435,39 +485,49 @@
     h0 = find(pos0, s0, 0)
     orig = jnp.where(h0 >= 0, h0, pos0)
     moved0, moved1 = pos0 != mine, pos1 != mine
+    touched = orig != mine
+    q = jnp.arange(rows, dtype=jnp.int32)
     if packed:
-        touched = orig != mine
-        q = jnp.arange(rows, dtype=jnp.int32)
         place = jnp.sum(((q[None, :] < q[:, None]) & touched[None, :]).astype(jnp.int32), axis=1)
-        s = jnp.arange(patch, dtype=jnp.int32)
-        pick = (place[None, :] == s[:, None]) & touched[None, :]
+        place = jnp.where(touched, place, -1)
+        s = jnp.arange(PATCH, dtype=jnp.int32)
+        pick = place[None, :] == s[:, None]
+        to = jnp.max(jnp.where(pick, q[None, :], -1), axis=1)
         from0 = jnp.max(jnp.where(pick & moved0[None, :], pos0[None, :], 0), axis=1)
         from1 = jnp.max(jnp.where(pick & moved1[None, :], pos1[None, :], 0), axis=1)
+        from_slab = jnp.max(jnp.where(pick, orig[None, :], 0), axis=1)
     else:
         from0, from1 = pos0, pos1
-    corner = jnp.concatenate([
-        g_panel[:width, 0:depth],
-        g_panel[width:2 * width, depth:2 * depth],
-        g_panel[2 * width:3 * width, 2 * depth:3 * depth],
-        jnp.take(g_panel, g1, axis=0)[:, 0:depth],
-        jnp.take(g_panel, row20, axis=0)[:, 0:depth],
-        jnp.take(g_panel, g2, axis=0)[:, depth:2 * depth],
-        jnp.take(g_panel, from0, axis=0)[:, 0:depth],
-        jnp.take(g_panel, from1, axis=0)[:, depth:2 * depth],
-    ]).T
-    g_slab, factor = exchange(slab, slab_piece, corner, tops, owners, ident + 1)
-
-    t = jnp.take(g_slab, take_t, axis=0)
-    kept = jnp.take(g_slab, jnp.where(orig != mine, orig, 0), axis=0)
-    base = jnp.where((orig != mine)[:, None], kept, slab)
-    left = []
-    for k, moved in ((0, moved0), (1, moved1)):
-        new = factor[:, 2 * top + k * patch:2 * top + (k + 1) * patch]
-        if packed:
-            new = jnp.dot(new, pick.astype(jnp.float32), precision=HIGHEST, preferred_element_type=jnp.float32)
-        left.append(jnp.where(moved[None, :], new, full[:, k * rows:(k + 1) * rows]))
-    left.append(full[:, 2 * rows:3 * rows])
-    return factor[:, :2 * top + 2 * 128], t, base, left
+
+    def block(index, k):
+        return rows_of(g_panel, index)[:, k * depth:(k + 1) * depth].T
+
+    corner = [g_panel[k * width:(k + 1) * width, k * depth:(k + 1) * depth].T for k in range(ticks)]
+    corner += [block(g1, 0), block(row20, 0), block(g2, 1)]
+    if packed:
+        wide = jnp.zeros((depth, width - 2 * PATCH), jnp.float32)
+        corner += [jnp.concatenate([block(from0, 0), block(from1, 1), wide], axis=1)]
+    else:
+        corner += [block(from0, 0), block(from1, 1)]
+    g_slab, factor = exchange(slab, slab_piece, jnp.stack(corner), tops, owners, ident + 1, LAG, CHUNKS, space)
+    t = rows_of(g_slab, take_t)
+    if packed:
+        base, replaced = slab, rows_of(g_slab, from_slab)
+        moved = jnp.stack([moved0, moved1] + [touched] * 6).astype(jnp.int32)
+    else:
+        base = jnp.where(touched[:, None], rows_of(g_slab, orig), slab)
+        full = jnp.stack([
+            jnp.where(moved0[None, :], factor[2 * ticks], full[0]),
+            jnp.where(moved1[None, :], factor[2 * ticks + 1], full[1]),
+            full[2],
+        ])
+        factor = factor[:2 * ticks + 1]
+        moved = jnp.zeros((8, rows), jnp.int32)
+        place, to = jnp.full((rows,), -1, jnp.int32), jnp.full((PATCH,), -1, jnp.int32)
+        replaced = jnp.zeros((PATCH, cols), jnp.float32)
+    ints = jnp.concatenate([to, jnp.full((8,), me, jnp.int32)])
+    place = jnp.broadcast_to(place[None, :], (8, rows))
+    return factor, full, t, base, replaced, ints, place, moved
 
 
 def solution(mesh):
@@ -475,23 +535,16 @@
 
     def local(slab, panels, pivots):
         rows, ticks = slab.shape[0], pivots.shape[0]
-        _, owner, rank = packing(pivots, rows)
+        packs = packing(pivots, rows)
+        _, owner, rank = packs
         fits = jnp.all((owner < ticks) | (rank < SLOTS))
-        factor, t, base, left = lax.cond(
+        ready = update(True, owners, slab, panels, pivots, packs)
+        return lax.cond(
             fits,
-            functools.partial(update, True, owners),
-            functools.partial(update, False, owners),
-            slab, panels, pivots,
+            lambda ready, rest: finish(ticks, *ready),
+            lambda ready, rest: finish(ticks, *update(False, owners, *rest)),
+            ready, (slab, panels, pivots, packs),
         )
-        width = pivots.shape[1]
-        upper = solve(factor, t, ticks, width)
-        me = lax.axis_index("row")
-        lowered = base
-        for k in range(ticks):
-            lowered = lowered - contract(left[k], upper[k * width:(k + 1) * width])
-        for k in range(ticks):
-            lowered = jnp.where(me == k, upper[k * width:(k + 1) * width], lowered)
-        return lowered
 
     in_specs = (P("row", "col"), P(None, "row", "col"), P())
     return jax.shard_map(local, mesh=mesh, in_specs=in_specs, out_specs=P("row", "col"), check_vma=False)

time: 238 us -> 167 us (0.70)
  the two profiles are of different devices: /device:TPU:257 before, /device:TPU:64 now
where the time goes in v2:
time: 167 us
  Pallas kernels  126 us (75%)
  local copies, waits for them, and re-layouts  31.9 us (19%)
  other arithmetic  7.5 us (4%)
    pallas_call x2, Pallas kernels, exchange(): pl.pallas_call(functools.partial(exchange_kernel, tops, z_size, lag, chun...  108 us
    gather x9, local copies, waits for them, and re-layouts, rows_of(): return jnp.take(array, index, axis=0, mode='clip')  21 us
    pallas_call x1, Pallas kernels, finish(): pl.pallas_call(functools.partial(finish_kernel, ticks), out_shape=jax.Sha...  18.8 us
    unnamed x28, local copies, waits for them, and re-layouts  4.93 us

profile of v2, /device:TPU:64, one launch (start us, length us, event | category | flops | bytes accessed | tf_op | source)
XLA Modules:
  0.0 166.8 jit_solution(12056823928347975158)
XLA Ops:
  0.1 0.8 fusion.30
  0.9 0.3 select_reduce_fusion.12
  1.2 0.6 select_reduce_fusion.11
  1.8 0.5 select_reduce_fusion.8
  2.8 0.7 reshape.416
  3.5 2.7 %convert_reduce_fusion = s32[1536]{0:T(1024)S(1)} fusion(s32[1536]{0:T(1024)S(1)} %add_select_fusion), kind=kLoop, calls=%fused_computation.69 | loop fusion | flops 11794944 | bytes 12288 | tf_op jit(solution)/shard_map/reduce_sum | solution.py:441
  6.2 1.4 or_reduce_fusion
  8.3 0.2 select_reduce_fusion.14
  8.5 2.3 %gather_fusion.9 = f32[64,256]{1,0:T(8,128)} fusion(f32[512,256]{1,0:T(8,128)} %top_ref.1, s32[1024]{0:T(1024)S(1)} %get-tuple-element.191), kind=kCustom, calls=%fused_computation.9 | custom fusion | bytes 131328 | tf_op jit(solution)/shard_map/jit(_take)/gather | solution.py:445
  10.9 0.9 fusion.28
  12.2 0.2 maximum_maximum_fusion.1.top_ref
  12.4 1.2 gather_fusion.10
  13.6 0.7 broadcast_in_dim.286
  14.3 49.2 %shard_map.39 = (f32[3584,128]{1,0:T(8,128)}, f32[3,16,32,512]{3,2,1,0:T(8,128)}) custom-call(f32[512,128]{1,0:T(8,128)} %copy-done.5, f32[64,128]{1,0:T(8,128)} %gather_fusion.10, f32[3,32,512]{2,1,0:T(8,128)S(1)} %bitcast.123), custom_call_target="tpu_custom_call" | custom-call | tf_op jit(solution)/shard_map/pallas_call | solution.py:313
  63.5 2.3 %gather_fusion.14 = f32[128,128]{1,0:T(8,128)S(1)} fusion(f32[3584,128]{1,0:T(8,128)} %get-tuple-element.115, s32[1024]{0:T(1024)S(1)} %get-tuple-element.187), kind=kCustom, calls=%fused_computation.14 | custom fusion | bytes 131584 | tf_op jit(solution)/shard_map/jit(_take)/gather | solution.py:445
  65.9 2.2 %gather_fusion.15 = f32[128,128]{1,0:T(8,128)S(1)} fusion(f32[3584,128]{1,0:T(8,128)} %get-tuple-element.115, s32[1024]{0:T(1024)S(1)} %get-tuple-element.186), kind=kCustom, calls=%fused_computation.15 | custom fusion | bytes 131584 | tf_op jit(solution)/shard_map/jit(_take)/gather | solution.py:445
  68.2 2.6 %gather_fusion.13 = f32[512,128]{1,0:T(8,128)S(1)} fusion(f32[3584,128]{1,0:T(8,128)} %get-tuple-element.115, s32[1024]{0:T(1024)S(1)} %get-tuple-element.188), kind=kCustom, calls=%fused_computation.13 | custom fusion | bytes 526336 | tf_op jit(solution)/shard_map/jit(_take)/gather | solution.py:445
  71.0 1.0 gather_fusion.12
  72.1 1.0 gather_fusion.11
  73.2 1.7 %copy.64 = f32[3584,128]{0,1:T(8,128)} copy(f32[3584,128]{1,0:T(8,128)S(1)} %copy-done) | data formatting | bytes 3670016 | tf_op jit(solution)/shard_map/pallas_call | solution.py:313
  75.0 0.9 fusion.11
  75.9 0.8 fusion.10
  76.7 0.8 fusion.9
  77.6 0.8 copy-done.7
  78.4 58.4 %shard_map.40 = (f32[3584,256]{1,0:T(8,128)}, f32[7,16,32,512]{3,2,1,0:T(8,128)}) custom-call(f32[512,256]{1,0:T(8,128)S(1)} %copy-done.1, f32[64,256]{1,0:T(8,128)} %gather_fusion.9, f32[7,32,512]{2,1,0:T(8,128)} %copy-done.7), custom_call_target="tpu_custom_call" | custom-call | tf_op jit(solution)/shard_map/pallas_call | solution.py:313
  136.7 0.7 broadcast_in_dim.279
  137.5 28.5 %conditional.1 = (f32[512,256]{1,0:T(8,128)S(1)}) conditional(s32[]{:T(128)} %convert_element_type.13, (f32[3,512,32]{1,2,0:T(8,128)S(1)}, s32[1536]{0:T(1024)S(1)}, s32[3,512]{1,0:T(4,128)S(1)}, f32[512,256]{1,0:T(8,128)S(1)}) %tuple.68, (f32[7,16,32,512]{3,2,1,0:T(8,128)}, f32[3,16,32,512]{3,2,1,0:T(8,128)}, s32[1536]{0:T(1024)S(1)}, ...), branch_computations={%region_12.19_spmd, %region_19.22_spmd} | conditional | flops 7166980 | bytes 76974024 | solution.py:542
  137.5 1.2 select_reduce_fusion.6
  138.7 2.8 %gather_fusion.1 = f32[128,256]{1,0:T(8,128)S(1)} fusion(f32[3584,256]{1,0:T(8,128)} %get-tuple-element.101, s32[1024]{0:T(1024)S(1)} %pad_clamp_fusion.8), kind=kCustom, calls=%fused_computation.8 | custom fusion | bytes 262656 | tf_op jit(solution)/shard_map/jit(_take)/gather | solution.py:445
  141.5 5.7 %gather_fusion = f32[1536,256]{1,0:T(8,128)S(1)} fusion(f32[3584,256]{1,0:T(8,128)} %get-tuple-element.101, s32[2048]{0:T(1024)S(1)} %pad_clamp_fusion.7), kind=kCustom, calls=%fused_computation.7 | custom fusion | bytes 3151872 | tf_op jit(solution)/shard_map/jit(_take)/gather | solution.py:445
  147.2 18.8 %branch_1_fun.2 = f32[512,256]{1,0:T(8,128)S(1)} custom-call(f32[7,512,512]{2,1,0:T(8,128)} %bitcast.120, f32[3,512,512]{2,1,0:T(8,128)} %bitcast.122, f32[1536,256]{1,0:T(8,128)S(1)} %gather_fusion, f32[512,256]{1,0:T(8,128)S(1)} %get-tuple-element.103.base_ref, f32[128,256]{1,0:T(8,128)S(1)} %gather_fusion.1, s32[136]{0:T(256)S(1)} %concatenate.17.ints_ref, ...), custom_call_target="tpu_custom_call" | custom-call | tf_op jit(solution)/shard_map/cond/branch_1_fun/pallas_call | solution.py:419
  166.0 0.8 copy-done.8
  (59 shorter events, 1.8 us)
Async XLA Ops:
  0.0 14.3 %copy-start.4 = (f32[3,512,32]{1,2,0:T(8,128)S(1)}, f32[3,512,32]{1,2,0:T(8,128)}, u32[]{:S(2)}) copy-start(f32[3,512,32]{1,2,0:T(8,128)} %param.6) | copy-start | bytes 589828
  12.4 1.9 %copy-start.5 = (f32[512,128]{1,0:T(8,128)}, f32[512,128]{1,0:T(8,128)S(1)}, u32[]{:S(2)}) copy-start(f32[512,128]{1,0:T(8,128)S(1)} %maximum_maximum_fusion.1.top_ref) | copy-start | bytes 786436
  63.5 7.4 %copy-start = (f32[3584,128]{1,0:T(8,128)S(1)}, f32[3584,128]{1,0:T(8,128)}, u32[]{:S(2)}) copy-start(f32[3584,128]{1,0:T(8,128)} %get-tuple-element.115) | copy-start | bytes 5505028
  72.1 6.2 %copy-start.1 = (f32[512,256]{1,0:T(8,128)S(1)}, f32[512,256]{1,0:T(8,128)}, u32[]{:S(2)}) copy-start(f32[512,256]{1,0:T(8,128)} %top_ref.1) | copy-start | bytes 1572868
  73.2 64.3 %copy-start.9 = (s32[3,512]{1,0:T(4,128)S(1)}, s32[3,512]{1,0:T(4,128)}, u32[]{:S(2)}) copy-start(s32[3,512]{1,0:T(4,128)} %param.7) | copy-start | bytes 18436
  77.6 0.8 copy-start.7
  166.0 0.8 copy-start.8

commit v3 on v0

v3 whole, which is shorter than its diff:
```python
import functools

import jax
import jax.numpy as jnp
from jax import lax
from jax.experimental import pallas as pl
from jax.experimental.pallas import tpu as pltpu
from jax.sharding import PartitionSpec as P

MESH = pl.DeviceIdType.MESH
SIDE = 4
SLOTS = 64
CHUNKS = 8
LAG = 4
SPREAD = 16
TILE = 128
PATCH = 128


def split(a):
    high = a.astype(jnp.bfloat16)
    return high, (a - high.astype(jnp.float32)).astype(jnp.bfloat16)


def mul(a, b):
    dot = functools.partial(jnp.dot, preferred_element_type=jnp.float32)
    (ah, al), (bh, bl) = split(a), split(b)
    return dot(ah, bh) + (dot(ah, bl) + dot(al, bh))


def remote(src, dst, send, recv, device):
    return pltpu.make_async_remote_copy(
        src_ref=src, dst_ref=dst, send_sem=send, recv_sem=recv, device_id=device, device_id_type=MESH
    )


class Place:
    def __init__(self, z_size):
        self.row, self.col = lax.axis_index("row"), lax.axis_index("col")
        self.z, self.core, self.z_size = self.row // 2, self.row % 2, z_size
        self.xx, self.yy = self.col // SIDE, self.col % SIDE
        self.up = (2 * ((self.z + 1) % z_size) + self.core, self.col)
        self.down = (2 * ((self.z + z_size - 1) % z_size) + self.core, self.col)
        self.partner = (2 * self.z + 1 - self.core, self.col)

    def side(self, step_x, step_y):
        return (self.row, ((self.xx + step_x) % SIDE) * SIDE + (self.yy + step_y) % SIDE)

    def greet(self):
        barrier = pltpu.get_barrier_semaphore()
        near = (self.up, self.down, self.partner)
        near += (self.side(1, 0), self.side(SIDE - 1, 0), self.side(0, 1), self.side(0, SIDE - 1))
        for device in near:
            pl.semaphore_signal(barrier, inc=1, device_id=device, device_id_type=MESH)
        pl.semaphore_wait(barrier, len(near))


class Ring:
    def __init__(self, place, tops, top_ref, piece_ref, g_ref, sems):
        self.p, self.tops, self.top_ref, self.piece_ref, self.g = place, tops, top_ref, piece_ref, g_ref
        (self.up_s, self.up_r, self.down_s, self.down_r, self.pr_s, self.pr_r,
         self.top_r, self.tu_s, self.td_s, self.tc_s, self.loc) = sems
        self.count, self.height = piece_ref.shape[0], top_ref.shape[0]
        self.chunk = self.height // CHUNKS
        self.ups = place.z_size // 2
        self.downs = place.z_size - 1 - self.ups
        self.total = LAG * self.ups + (CHUNKS if tops else 1)

    def slot(self, z, core):
        at = self.tops * self.height + (2 * (z % self.p.z_size) + core) * self.count
        return self.g.at[pl.ds(pl.multiple_of(at, 8), self.count), :]

    def hop(self, s, way, got=False):
        back = s + 1 if got else s
        if way == "up":
            ref = self.slot(self.p.z + self.p.z_size - back, self.p.core)
            return remote(ref, ref, self.up_s.at[s], self.up_r.at[s], self.p.up)
        ref = self.slot(self.p.z + back, self.p.core)
        return remote(ref, ref, self.down_s.at[s], self.down_r.at[s], self.p.down)

    def share(self, hops, got=False):
        core = 1 - self.p.core if got else self.p.core
        ref = self.slot(self.p.z + self.p.z_size - hops, core)
        return remote(ref, ref, self.pr_s.at[hops], self.pr_r.at[hops], self.p.partner)

    def top_roles(self, b):
        h = (self.p.z + self.p.z_size - b // 2) % self.p.z_size
        hops = jnp.where(h <= self.ups, h, self.p.z_size - h)
        mine = self.p.core == b % 2
        return mine, mine & (h < self.ups), mine & ((h == 0) | (h > self.ups + 1)), mine & (h > 0), hops

    def top_copy(self, b, i, kind):
        ref = self.g.at[pl.ds(pl.multiple_of(b * self.height + i * self.chunk, 8), self.chunk), :]
        send, device = {
            "up": (self.tu_s, self.p.up), "down": (self.td_s, self.p.down), "core": (self.tc_s, self.p.partner)
        }[kind]
        return remote(ref, ref, send.at[b, i], self.top_r.at[b, i], device)

    def place_own(self):
        own = pltpu.make_async_copy(self.piece_ref, self.slot(self.p.z, self.p.core), self.loc.at[0])
        own.start()
        for b in range(self.tops):
            @pl.when(self.p.row == b)
            def _():
                to = self.g.at[pl.ds(b * self.height, self.height), :]
                top = pltpu.make_async_copy(self.top_ref, to, self.loc.at[1])
                top.start()
                top.wait()
        own.wait()

    def begin(self):
        self.hop(0, "up").start()
        self.hop(0, "down").start()
        self.share(0).start()

    def step(self, t):
        for b in range(self.tops):
            mine, to_up, to_down, gets, hops = self.top_roles(b)
            i = t - LAG * hops
            inside = (i >= 0) & (i < CHUNKS)

            @pl.when(inside & gets)
            def _():
                self.top_copy(b, i, "up").wait_recv()

            @pl.when(inside & to_up)
            def _():
                self.top_copy(b, i, "up").start()

            @pl.when(inside & to_down)
            def _():
                self.top_copy(b, i, "down").start()

            @pl.when(inside & mine)
            def _():
                self.top_copy(b, i, "core").start()

        s = t // LAG
        now = (t % LAG == 0) & (s >= 1)

        @pl.when(now & (s <= self.ups))
        def _():
            self.hop(s - 1, "up", True).wait_recv()

            @pl.when(s < self.ups)
            def _():
                self.hop(s, "up").start()

            self.share(s).start()

        @pl.when(now & (s <= self.downs))
        def _():
            self.hop(s - 1, "down", True).wait_recv()

            @pl.when(s < self.downs)
            def _():
                self.hop(s, "down").start()

            self.share(self.p.z_size - s).start()

    def gather(self):
        def rest(s, carry):
            self.share(s, True).wait_recv()
            return carry

        lax.fori_loop(0, self.p.z_size, rest, 0)

        def chunks(i, carry):
            for b in range(self.tops):
                @pl.when(jnp.logical_not(self.top_roles(b)[0]))
                def _():
                    self.top_copy(b, i, "core").wait_recv()

            return carry

        if self.tops:
            lax.fori_loop(0, CHUNKS, chunks, 0)

    def drain(self):
        def hops(way):
            def body(s, carry):
                self.hop(s, way).wait_send()
                return carry

            return body

        def shares(s, carry):
            self.share(s).wait_send()
            return carry

        lax.fori_loop(0, self.ups, hops("up"), 0)
        lax.fori_loop(0, self.downs, hops("down"), 0)
        lax.fori_loop(0, self.p.z_size, shares, 0)

        def chunks(i, carry):
            for b in range(self.tops):
                mine, to_up, to_down, _, _ = self.top_roles(b)
                for role, kind in ((to_up, "up"), (to_down, "down"), (mine, "core")):
                    @pl.when(role)
                    def _():
                        self.top_copy(b, i, kind).wait_send()

            return carry

        if self.tops:
            lax.fori_loop(0, CHUNKS, chunks, 0)


def ring_sems(z_size, tops):
    dma, blocks = pltpu.SemaphoreType.DMA, max(tops, 1)
    return [dma((z_size,))] * 6 + [dma((blocks, CHUNKS))] * 4 + [dma((2,))]


class Torus:
    def __init__(self, place, blocks, x_ref, xo_ref, sems):
        self.p, self.blocks, self.x, self.xo = place, blocks, x_ref, xo_ref
        self.s, self.r, self.loc = sems
        self.half, self.quarter = x_ref.shape[1] // 2, x_ref.shape[1] // 4

    def place_own(self):
        return pltpu.make_async_copy(
            self.x.at[self.blocks], self.xo.at[self.blocks, self.p.xx, self.p.yy], self.loc.at[0]
        )

    def piece(self, k, first, second, part):
        x, y = (first, second) if k == 0 else (second, first)
        start, size = {"all": (0, self.half), "low": (0, self.quarter), "high": (self.quarter, self.quarter)}[part]
        return self.xo.at[
            self.blocks, (self.p.xx + x) % SIDE, (self.p.yy + y) % SIDE, pl.ds(k * self.half + start, size), :
        ]

    def copy(self, k, stage, v, e, receive=False):
        first = (0, SIDE - 1, 1, 2)[v]
        there, part = {0: (0, "all"), 1: (0, "all"), 2: (SIDE - 1, "low"), 3: (1, "high")}[e]
        here = (SIDE - 1, 1, 2, 2)[e]
        step = 1 if e in (0, 2) else SIDE - 1
        device = self.p.side(step, 0) if (k == 0) == (stage == 0) else self.p.side(0, step)
        n = (k * 5 + (0 if stage == 0 else 1 + v)) * 4 + e
        at = here if receive else there
        ref = self.piece(k, at, 0, part) if stage == 0 else self.piece(k, first, at, part)
        src = ref
        if e < 2 and (stage == 0 or v == 0) and not receive:
            src = self.x.at[self.blocks, pl.ds(k * self.half, self.half), :]
        return remote(src, ref, self.s.at[n], self.r.at[n], device)

    def start(self, stage, v, es):
        for e in es:
            for k in range(2):
                self.copy(k, stage, v, e).start()

    def arrive(self, stage, v, e):
        for k in range(2):
            self.copy(k, stage, v, e, True).wait_recv()

    def begin(self):
        self.start(0, 0, (0, 1))
        self.start(1, 0, (0, 1))

    def pass_on(self, stage, v):
        self.arrive(stage, v, 0)
        self.start(stage, v, (2,))
        self.arrive(stage, v, 1)
        self.start(stage, v, (3,))

    def event(self, number):
        if number == 0:
            self.arrive(0, 0, 0)
            self.start(0, 0, (2,))
            self.start(1, 1, (0, 1))
            self.arrive(0, 0, 1)
            self.start(0, 0, (3,))
            self.start(1, 2, (0, 1))
        elif number == 1:
            self.pass_on(1, 0)
        elif number == 2:
            self.arrive(0, 0, 2)
            self.arrive(0, 0, 3)
            self.start(1, 3, (0, 1))
        elif number < 6:
            self.pass_on(1, number - 2)

    def complete(self, v):
        self.arrive(1, v, 2)
        self.arrive(1, v, 3)

    def drain(self):
        for k in range(2):
            for e in range(4):
                self.copy(k, 0, 0, e).wait_send()
                for v in range(4):
                    self.copy(k, 1, v, e).wait_send()


def torus_sems():
    return [pltpu.SemaphoreType.DMA((40,))] * 2 + [pltpu.SemaphoreType.DMA((1,))]


def run(begin, end, *steps):
    def body(t, carry):
        for step in steps:
            step(t)
        return carry

    lax.fori_loop(begin, end, body, 0)


def plain_kernel(z_size, piece_ref, x_ref, g_ref, xo_ref, *sems):
    place = Place(z_size)
    place.greet()
    ring = Ring(place, 0, piece_ref, piece_ref, g_ref, sems[:11])
    torus = Torus(place, pl.ds(0, x_ref.shape[0]), x_ref, xo_ref, sems[11:])
    own = torus.place_own()
    own.start()
    torus.begin()
    ring.place_own()
    ring.begin()
    own.wait()
    run(0, ring.total, ring.step)
    for number in range(6):
        torus.event(number)
    for v in range(4):
        torus.complete(v)
    ring.gather()
    ring.drain()
    torus.drain()


def exchange(piece, x, owners, ident):
    vmem, hbm = pl.BlockSpec(memory_space=pltpu.VMEM), pl.BlockSpec(memory_space=pl.ANY)
    g, xo = pl.pallas_call(
        functools.partial(plain_kernel, owners // 2),
        out_shape=(
            jax.ShapeDtypeStruct((owners * piece.shape[0], piece.shape[1]), jnp.float32),
            jax.ShapeDtypeStruct((x.shape[0], SIDE, SIDE) + x.shape[1:], jnp.float32),
        ),
        in_specs=[vmem, vmem],
        out_specs=(hbm, hbm),
        scratch_shapes=ring_sems(owners // 2, 0) + torus_sems(),
        compiler_params=pltpu.CompilerParams(collective_id=ident, has_side_effects=True),
    )(piece, x)
    return g, xo.reshape(x.shape[0], SIDE * SIDE * x.shape[1], x.shape[2])


def packed_kernel(ticks, z_size, index_ref, ptop_ref, ppiece_ref, stop_ref, spiece_ref, x_ref,
                  gs_ref, full_ref, f_ref, gp_ref, rows_ref, y_ref, sh_s, sh_r, *sems):
    place = Place(z_size)
    place.greet()
    panel = Ring(place, ticks, ptop_ref, ppiece_ref, gp_ref, sems[:11])
    slab = Ring(place, ticks, stop_ref, spiece_ref, gs_ref, sems[11:22])
    torus = Torus(place, pl.ds(0, ticks), x_ref, full_ref, sems[22:25])
    mine = (ticks + 1) * place.core
    corner = Torus(place, pl.ds(mine, ticks + 1), y_ref, f_ref, sems[25:])
    depth, width = y_ref.shape[1:]

    own = torus.place_own()
    own.start()
    torus.begin()
    panel.place_own()
    panel.begin()
    slab.place_own()
    own.wait()
    total = panel.total
    shift = total - SPREAD
    begin = 0
    for number in range(7):
        end = total if number == 6 else 2 + (total - 2) * number // 6
        for low, high, both in ((begin, min(end, shift), False), (max(begin, shift), end, True)):
            if low < high:
                if both and low == shift:
                    slab.begin()
                steps = (panel.step,) + ((lambda t: slab.step(t - shift),) if both else ())
                run(low, high, *steps)
        begin = end
        torus.event(number)
    panel.gather()

    def load(i, carry):
        for n in range(8):
            at = i * 8 + n
            rows_ref[pl.ds(at, 1), :] = gp_ref[pl.ds(index_ref[at], 1), :]
        return carry

    lax.fori_loop(0, rows_ref.shape[0] // 8, load, 0)
    for k in range(ticks):
        y_ref[k] = gp_ref[pl.ds(k * width, width), :].T[k * depth:(k + 1) * depth]
    for n, k in ((0, 0), (1, 0), (2, 1)):
        y_ref[ticks + 1 + n] = rows_ref[pl.ds(n * width, width), :].T[k * depth:(k + 1) * depth]
    patches = rows_ref[pl.ds(3 * width, 2 * PATCH), :].T
    zeros = jnp.zeros((depth, width - 2 * PATCH), jnp.float32)
    y_ref[mine + ticks] = jnp.concatenate([patches[:depth, :PATCH], patches[depth:2 * depth, PATCH:], zeros], axis=1)

    run(total, total + 2, lambda t: slab.step(t - shift))
    own = corner.place_own()
    own.start()
    corner.begin()
    own.wait()
    begin, last = total + 2, total + shift

    def pass_share(k, v, receive=False):
        first = (0, SIDE - 1, 1, 2)[v]
        to = pl.ds((ticks + 1) * (1 - place.core if receive else place.core), ticks)
        half = pl.ds(k * corner.half, corner.half)
        if k == 0:
            ref = f_ref.at[to, (place.xx + first) % SIDE, :, half, :]
        else:
            ref = f_ref.at[to, :, (place.yy + first) % SIDE, half, :]
        return remote(ref, ref, sh_s.at[k, v], sh_r.at[k, v], place.partner)

    for number in range(7):
        end = last if number == 6 else begin + (last - begin) // (7 - number)
        if begin < end:
            run(begin, end, lambda t: slab.step(t - shift))
        begin = end
        corner.event(number)
        if number >= 4:
            v = number - 4
            corner.complete(v)
            for k in range(2):
                pass_share(k, v).start()
    corner.complete(3)
    for k in range(2):
        pass_share(k, 3).start()
    slab.gather()
    for v in range(4):
        torus.complete(v)
    for v in range(4):
        for k in range(2):
            pass_share(k, v, True).wait_recv()
            pass_share(k, v).wait_send()
    panel.drain()
    slab.drain()
    torus.drain()
    corner.drain()


def packed_exchange(index, ptop, ppiece, stop, spiece, x, ticks, owners, ident):
    vmem = pl.BlockSpec(memory_space=pltpu.VMEM)
    z_size, blocks = owners // 2, 2 * (ticks + 1)
    packed = ticks * ptop.shape[0] + owners * ppiece.shape[0]
    torus = (SIDE, SIDE) + x.shape[1:]
    f32 = jnp.float32
    gs, full, f = pl.pallas_call(
        functools.partial(packed_kernel, ticks, z_size),
        out_shape=(
            jax.ShapeDtypeStruct((packed, stop.shape[1]), f32),
            jax.ShapeDtypeStruct((ticks,) + torus, f32),
            jax.ShapeDtypeStruct((blocks,) + torus, f32),
        ),
        in_specs=[pl.BlockSpec(memory_space=pltpu.SMEM)] + [vmem] * 5,
        out_specs=(vmem, vmem, vmem),
        scratch_shapes=[
            pltpu.VMEM((packed, ptop.shape[1]), f32),
            pltpu.VMEM((index.shape[0], ptop.shape[1]), f32),
            pltpu.VMEM((blocks,) + x.shape[1:], f32),
            pltpu.SemaphoreType.DMA((2, 4)), pltpu.SemaphoreType.DMA((2, 4)),
        ] + ring_sems(z_size, ticks) * 2 + torus_sems() * 2,
        compiler_params=pltpu.CompilerParams(collective_id=ident, has_side_effects=True),
    )(index, ptop, ppiece, stop, spiece, x)
    width, depth = x.shape[2], SIDE * SIDE * x.shape[1]
    return gs, full.reshape(ticks, depth, width), f.reshape(blocks, depth, width)


def invert_tiles(tiles):
    k = lax.broadcasted_iota(jnp.int32, tiles[0].shape, 0)
    r = lax.broadcasted_iota(jnp.int32, tiles[0].shape, 1)
    eye = jnp.where(k == r, 1.0, 0.0).astype(jnp.float32)
    strict = [jnp.where(k < r, tile, 0.0) for tile in tiles]
    power = [jnp.where(k // 16 == r // 16, -tile, 0.0) for tile in strict]
    inverse = [eye + tile for tile in power]
    for _ in range(3):
        power = [mul(tile, tile) for tile in power]
        inverse = [one + mul(one, tile) for one, tile in zip(inverse, power)]
    for size in (16, 32, 64):
        pick = (k // (2 * size) == r // (2 * size)) & (k // size != r // size)
        half = [mul(jnp.where(pick, tile, 0.0), one) for tile, one in zip(strict, inverse)]
        inverse = [one - mul(one, tile) for one, tile in zip(inverse, half)]
    return inverse


def finish_kernel(ticks, f_ref, full_ref, t_ref, base_ref, touched_ref, ints_ref, place_ref, moved_ref,
                  out_ref, inv_ref, u_ref):
    width = f_ref.shape[1]
    tiles = width // TILE
    inv_ref[...] = jnp.zeros_like(inv_ref)

    def invert(b, carry):
        spots = [pl.ds(j * TILE, TILE) for j in range(tiles)]
        for spot, one in zip(spots, invert_tiles([f_ref[b, spot, spot] for spot in spots])):
            inv_ref[b, spot, spot] = one
        return carry

    lax.fori_loop(0, ticks, invert, 0)
    size = TILE
    while size < width:
        spots = [
            (b, pl.ds(low, size), pl.ds(low + size, size))
            for b in range(ticks) for low in range(0, width, 2 * size)
        ]
        half = [mul(f_ref[b, near, far], inv_ref[b, far, far]) for b, near, far in spots]
        for (b, near, far), tile in zip(spots, half):
            inv_ref[b, near, far] = -mul(inv_ref[b, near, near], tile)
        size *= 2

    off = ticks + 1
    for b in range(ticks):
        rhs = t_ref[pl.ds(b * width, width), :].T
        for j in range(b):
            rhs = rhs - mul(u_ref[j], f_ref[off])
            off += 1
        u_ref[b] = mul(rhs, inv_ref[b])

    me = ints_ref[PATCH]

    @pl.when(me < ticks)
    def _():
        out_ref[...] = u_ref[jnp.minimum(me, ticks - 1)].T

    @pl.when(me >= ticks)
    def _():
        out_ref[...] = base_ref[...]

        def place_row(s, carry):
            to = ints_ref[s]

            @pl.when(to >= 0)
            def _():
                out_ref[pl.ds(to, 1), :] = touched_ref[pl.ds(s, 1), :]

            return carry

        lax.fori_loop(0, PATCH, place_row, 0)
        s = lax.broadcasted_iota(jnp.int32, (PATCH, place_ref.shape[1]), 0)
        pick = jnp.where(place_ref[0:1, :] == s, 1.0, 0.0).astype(jnp.bfloat16)
        total = None
        for k in range(ticks):
            left = full_ref[k]
            if k < ticks - 1:
                high, low = split(f_ref[ticks + (ticks + 1) * (me % 2), :, pl.ds(k * PATCH, PATCH)])
                new = jnp.dot(high, pick, preferred_element_type=jnp.float32)
                new = new + jnp.dot(low, pick, preferred_element_type=jnp.float32)
                left = jnp.where(moved_ref[k:k + 1, :] > 0, new, left)
            part = mul(u_ref[k], left)
            total = part if total is None else total + part
        out_ref[...] = out_ref[...] - total.T


def finish(ticks, factor, full, t, base, touched, ints, place, moved):
    vmem = pl.BlockSpec(memory_space=pltpu.VMEM)
    width, cols = factor.shape[1], t.shape[1]
    return pl.pallas_call(
        functools.partial(finish_kernel, ticks),
        out_shape=jax.ShapeDtypeStruct(base.shape, jnp.float32),
        in_specs=[vmem] * 5 + [pl.BlockSpec(memory_space=pltpu.SMEM), vmem, vmem],
        out_specs=vmem,
        scratch_shapes=[
            pltpu.VMEM((ticks, width, width), jnp.float32), pltpu.VMEM((ticks, cols, width), jnp.float32)
        ],
        compiler_params=pltpu.CompilerParams(vmem_limit_bytes=50 * 1024 * 1024),
    )(factor, full, t, base, touched, ints, place, moved)


def find(a, b, base):
    i = jnp.arange(b.shape[0], dtype=jnp.int32)
    return jnp.max(jnp.where(a[:, None] == b[None, :], base + i[None, :], -1), axis=1)


def packing(pivots, rows):
    src = pivots.reshape(-1)
    owner = src // rows
    e = jnp.arange(src.shape[0], dtype=jnp.int32)
    same = (owner[:, None] == owner[None, :]) & (e[None, :] < e[:, None])
    return src, owner, jnp.sum(same.astype(jnp.int32), axis=1)


def rows_of(array, index):
    return jnp.take(array, index, axis=0, mode="clip")


def update(packed, owners, slab, panels, pivots, packs):
    rows, cols = slab.shape
    ticks, width = pivots.shape
    depth = panels.shape[2]
    me = lax.axis_index("row")
    src, owner, rank = packs
    top = ticks * width
    panel_rows = jnp.concatenate(
        [panels[k] for k in range(ticks)] + [jnp.zeros((rows, 128 - ticks * depth), jnp.float32)], axis=1
    )
    g = src
    if packed:
        g = jnp.where(owner < ticks, src, top + jnp.minimum(owner * SLOTS + rank, owners * SLOTS - 1))
        s = jnp.arange(SLOTS, dtype=jnp.int32)
        held = (owner[None, :] == me) & (rank[None, :] == s[:, None])
        listed = jnp.max(jnp.where(held, src[None, :] - me * rows, 0), axis=1)
    x_panels = jnp.transpose(panels, (0, 2, 1))

    s0, s1, s2 = pivots
    g0, g1, g2 = g[:width], g[width:2 * width], g[2 * width:]
    back = find(s2, s1, width)
    f2 = find(jnp.where(back >= 0, back, s2), s0, 0)
    f1 = find(s1, s0, 0)
    row20 = jnp.where(back >= 0, back, g2)
    take_t = jnp.concatenate([g0, jnp.where(f1 >= 0, f1, g1), jnp.where(f2 >= 0, f2, row20)])
    mine = me * rows + jnp.arange(rows, dtype=jnp.int32)
    h2 = find(mine, s2, 2 * width)
    pos1 = jnp.where(h2 >= 0, h2, mine)
    h1 = find(pos1, s1, width)
    pos0 = jnp.where(h1 >= 0, h1, pos1)
    h0 = find(pos0, s0, 0)
    orig = jnp.where(h0 >= 0, h0, pos0)
    moved0, moved1 = pos0 != mine, pos1 != mine
    touched = orig != mine
    q = jnp.arange(rows, dtype=jnp.int32)
    if packed:
        place = jnp.sum(((q[None, :] < q[:, None]) & touched[None, :]).astype(jnp.int32), axis=1)
        place = jnp.where(touched, place, -1)
        s = jnp.arange(PATCH, dtype=jnp.int32)
        pick = place[None, :] == s[:, None]
        to = jnp.max(jnp.where(pick, q[None, :], -1), axis=1)
        from0 = jnp.max(jnp.where(pick & moved0[None, :], pos0[None, :], 0), axis=1)
        from1 = jnp.max(jnp.where(pick & moved1[None, :], pos1[None, :], 0), axis=1)
        from_slab = jnp.max(jnp.where(pick, orig[None, :], 0), axis=1)
    else:
        from0, from1 = pos0, pos1

    if packed:
        index = jnp.concatenate([g1, row20, g2, from0, from1])
        g_slab, full, factor = packed_exchange(
            index, panel_rows, rows_of(panel_rows, listed), slab, rows_of(slab, listed), x_panels, ticks, owners, 0
        )
        base, replaced = slab, rows_of(g_slab, from_slab)
        moved = jnp.stack([moved0, moved1] + [touched] * 6).astype(jnp.int32)
    else:
        g_panel, full = exchange(panel_rows, x_panels, owners, 1)

        def block(index, k):
            return rows_of(g_panel, index)[:, k * depth:(k + 1) * depth].T

        corner = [g_panel[k * width:(k + 1) * width, k * depth:(k + 1) * depth].T for k in range(ticks)]
        corner += [block(from0, 0), block(g1, 0), block(row20, 0), block(g2, 1), block(from1, 1)]
        g_slab, factor = exchange(slab, jnp.stack(corner), owners, 2)
        base = jnp.where(touched[:, None], rows_of(g_slab, orig), slab)
        full = jnp.stack([
            jnp.where(moved0[None, :], factor[ticks], full[0]),
            jnp.where(moved1[None, :], factor[2 * ticks + 1], full[1]),
            full[2],
        ])
        moved = jnp.zeros((8, rows), jnp.int32)
        place, to = jnp.full((rows,), -1, jnp.int32), jnp.full((PATCH,), -1, jnp.int32)
        replaced = jnp.zeros((PATCH, cols), jnp.float32)
    t = rows_of(g_slab, take_t)
    ints = jnp.concatenate([to, jnp.full((8,), me, jnp.int32)])
    place = jnp.broadcast_to(place[None, :], (8, rows))
    return factor, full, t, base, replaced, ints, place, moved


def solution(mesh):
    owners = mesh.shape["row"]

    def local(slab, panels, pivots):
        rows, ticks = slab.shape[0], pivots.shape[0]
        packs = packing(pivots, rows)
        _, owner, rank = packs
        fits = jnp.all((owner < ticks) | (rank < SLOTS))
        ready = update(True, owners, slab, panels, pivots, packs)
        return lax.cond(
            fits,
            lambda ready, rest: finish(ticks, *ready),
            lambda ready, rest: finish(ticks, *update(False, owners, *rest)),
            ready, (slab, panels, pivots, packs),
        )

    in_specs = (P("row", "col"), P(None, "row", "col"), P())
    return jax.shard_map(local, mesh=mesh, in_specs=in_specs, out_specs=P("row", "col"), check_vma=False)
```

time: 971 us -> 139 us (0.14)
  the two profiles are of different devices: /device:TPU:1 before, /device:TPU:64 now
where the time goes in v3:
time: 139 us; the launch traced here: 138 us
  Pallas kernels  112 us (81%)
  local copies, waits for them, and re-layouts  17.3 us (12%)
  other arithmetic  7.48 us (5%)
    pallas_call x1, Pallas kernels, packed_exchange(): pl.pallas_call(functools.partial(packed_kernel, ticks, z_size), out_shape...  93.4 us
    pallas_call x1, Pallas kernels, finish(): pl.pallas_call(functools.partial(finish_kernel, ticks), out_shape=jax.Sha...  19 us
    gather x4, local copies, waits for them, and re-layouts, rows_of(): return jnp.take(array, index, axis=0, mode='clip')  12 us

profile of v3, /device:TPU:64, one launch (start us, length us, event | category | flops | bytes accessed | tf_op | source)
XLA Modules:
  0.0 138.1 jit_solution(16916271209783983732)
XLA Ops:
  0.0 0.1 pad.20.clone
  0.1 0.8 fusion.25
  0.9 0.3 select_reduce_fusion.12
  1.2 0.6 select_reduce_fusion.11
  1.8 0.5 select_reduce_fusion.8
  2.3 0.2 convert_reduce_fusion.1
  2.5 0.2 select_reduce_fusion.15
  2.8 0.7 reshape.417
  3.5 2.7 %convert_reduce_fusion = s32[1536]{0:T(1024)S(1)} fusion(s32[1536]{0:T(1024)S(1)} %add_select_fusion), kind=kLoop, calls=%fused_computation.64 | loop fusion | flops 11794944 | bytes 12288 | tf_op jit(solution)/shard_map/reduce_sum | solution.py:572
  6.2 1.4 or_reduce_fusion
  8.3 0.2 select_reduce_fusion.14
  8.5 0.0 copy-start.8
  8.6 2.3 %gather_fusion.10 = f32[64,256]{1,0:T(8,128)} fusion(f32[512,256]{1,0:T(8,128)} %stop_ref.1, s32[1024]{0:T(1024)S(1)} %pad_clamp_fusion.9), kind=kCustom, calls=%fused_computation.10 | custom fusion | bytes 131328 | tf_op jit(solution)/shard_map/jit(_take)/gather | solution.py:576
  10.9 0.9 fusion.24
  11.8 0.1 copy.53
  12.0 0.1 copy.54
  12.1 0.1 copy.55
  12.2 0.2 maximum_maximum_fusion.1.ptop_ref
  12.4 0.0 copy-start.4
  12.5 1.2 gather_fusion.9
  13.6 0.7 broadcast_in_dim.260
  14.4 0.0 copy-done.8
  14.4 0.0 copy-done.4
  14.4 93.4 %shard_map.39 = (f32[3584,256]{1,0:T(8,128)}, f32[3,4,4,32,512]{4,3,2,1,0:T(8,128)}, f32[8,4,4,32,512]{4,3,2,1,0:T(8,128)}) custom-call(s32[1792]{0:T(1024)} %copy-done.8, f32[512,128]{1,0:T(8,128)} %copy-done.4, f32[64,128]{1,0:T(8,128)} %gather_fusion.9, f32[512,256]{1,0:T(8,128)S(1)} %copy-done, f32[64,256]{1,0:T(8,128)} %gather_fusion.10, ...), custom_call_target="tpu_custom_call" | custom-call | tf_op jit(solution)/shard_map/pallas_call | solution.py:442
  107.8 0.8 broadcast_in_dim.253
  108.5 28.8 %conditional.1 = (f32[512,256]{1,0:T(8,128)S(1)}) conditional(s32[]{:T(128)} %convert_element_type.13, (f32[3,512,32]{1,2,0:T(8,128)S(1)}, s32[3,512]{1,0:T(4,128)S(1)}, s32[1536]{0:T(1024)S(1)}, f32[512,256]{1,0:T(8,128)S(1)}) %tuple.63, (f32[8,4,4,32,512]{4,3,2,1,0:T(8,128)}, f32[3,4,4,32,512]{4,3,2,1,0:T(8,128)}, s32[1536]{0:T(1024)S(1)}, ...), branch_computations={%region_12.19_spmd, %region_19.22_spmd} | conditional | flops 7166980 | bytes 62293976 | solution.py:666
  108.5 1.2 select_reduce_fusion.6
  109.7 2.8 %gather_fusion.1 = f32[128,256]{1,0:T(8,128)S(1)} fusion(f32[3584,256]{1,0:T(8,128)} %get-tuple-element.101, s32[1024]{0:T(1024)S(1)} %pad_clamp_fusion.8), kind=kCustom, calls=%fused_computation.8 | custom fusion | bytes 262656 | tf_op jit(solution)/shard_map/jit(_take)/gather | solution.py:576
  112.5 5.7 %gather_fusion = f32[1536,256]{1,0:T(8,128)S(1)} fusion(f32[3584,256]{1,0:T(8,128)} %get-tuple-element.101, s32[2048]{0:T(1024)S(1)} %pad_clamp_fusion.7), kind=kCustom, calls=%fused_computation.7 | custom fusion | bytes 3151872 | tf_op jit(solution)/shard_map/jit(_take)/gather | solution.py:576
  118.2 19.0 %branch_1_fun.2 = f32[512,256]{1,0:T(8,128)S(1)} custom-call(f32[8,512,512]{2,1,0:T(8,128)} %bitcast.81, f32[3,512,512]{2,1,0:T(8,128)} %bitcast.83, f32[1536,256]{1,0:T(8,128)S(1)} %gather_fusion, f32[512,256]{1,0:T(8,128)S(1)} %get-tuple-element.103.base_ref, f32[128,256]{1,0:T(8,128)S(1)} %gather_fusion.1, s32[136]{0:T(256)S(1)} %concatenate.17.ints_ref, ...), custom_call_target="tpu_custom_call" | custom-call | tf_op jit(solution)/shard_map/cond/branch_1_fun/pallas_call | solution.py:550
  137.3 0.0 copy-start.6
  137.3 0.8 copy-done.6
  (36 shorter events, 0.3 us)
Async XLA Ops:
  0.0 108.5 %copy-start.7 = (s32[3,512]{1,0:T(4,128)S(1)}, s32[3,512]{1,0:T(4,128)}, u32[]{:S(2)}) copy-start(s32[3,512]{1,0:T(4,128)} %param.7) | copy-start | bytes 18436
  0.0 14.4 %copy-start = (f32[512,256]{1,0:T(8,128)S(1)}, f32[512,256]{1,0:T(8,128)}, u32[]{:S(2)}) copy-start(f32[512,256]{1,0:T(8,128)} %stop_ref.1) | copy-start | bytes 1572868
  0.0 14.4 %copy-start.3 = (f32[3,512,32]{1,2,0:T(8,128)S(1)}, f32[3,512,32]{1,2,0:T(8,128)}, u32[]{:S(2)}) copy-start(f32[3,512,32]{1,2,0:T(8,128)} %param.6) | copy-start | bytes 589828
  8.5 5.8 %copy-start.8 = (s32[1792]{0:T(1024)}, s32[1792]{0:T(1024)S(1)}, u32[]{:S(2)}) copy-start(s32[1792]{0:T(1024)S(1)} %constant_dynamic-update-slice_fusion.index_ref) | copy-start | bytes 21508
  12.4 1.9 %copy-start.4 = (f32[512,128]{1,0:T(8,128)}, f32[512,128]{1,0:T(8,128)S(1)}, u32[]{:S(2)}) copy-start(f32[512,128]{1,0:T(8,128)S(1)} %maximum_maximum_fusion.1.ptop_ref) | copy-start | bytes 786436
  137.3 0.8 copy-start.6

commit v4 on v3

--- a/solution.py
+++ b/solution.py
@@ -341,9 +341,22 @@
     return g, xo.reshape(x.shape[0], SIDE * SIDE * x.shape[1], x.shape[2])
 
 
-def packed_kernel(ticks, z_size, index_ref, ptop_ref, ppiece_ref, stop_ref, spiece_ref, x_ref,
-                  gs_ref, full_ref, f_ref, gp_ref, rows_ref, y_ref, sh_s, sh_r, *sems):
+def packed_kernel(ticks, z_size, index_ref, take_ref, stop_ref, x_ref, full_ref, f_ref, t_ref,
+                  ptop_ref, ppiece_ref, spiece_ref, gs_ref, gp_ref, rows_ref, y_ref, sh_s, sh_r, *sems):
     place = Place(z_size)
+    spare = jnp.zeros((ptop_ref.shape[1] - ticks * x_ref.shape[1], x_ref.shape[2]), jnp.float32)
+    ptop_ref[...] = jnp.concatenate([x_ref[k] for k in range(ticks)] + [spare], axis=0).T
+    first = rows_ref.shape[0]
+
+    def pack(i, carry):
+        for n in range(8):
+            at = i * 8 + n
+            row = index_ref[first + at]
+            ppiece_ref[pl.ds(at, 1), :] = ptop_ref[pl.ds(row, 1), :]
+            spiece_ref[pl.ds(at, 1), :] = stop_ref[pl.ds(row, 1), :]
+        return carry
+
+    lax.fori_loop(0, ppiece_ref.shape[0] // 8, pack, 0)
     place.greet()
     panel = Ring(place, ticks, ptop_ref, ppiece_ref, gp_ref, sems[:11])
     slab = Ring(place, ticks, stop_ref, spiece_ref, gs_ref, sems[11:22])
@@ -406,12 +419,21 @@
             ref = f_ref.at[to, :, (place.yy + first) % SIDE, half, :]
         return remote(ref, ref, sh_s.at[k, v], sh_r.at[k, v], place.partner)
 
+    def pick(i, carry):
+        for n in range(8):
+            at = i * 8 + n
+            t_ref[pl.ds(at, 1), :] = gs_ref[pl.ds(take_ref[at], 1), :]
+        return carry
+
     for number in range(7):
         end = last if number == 6 else begin + (last - begin) // (7 - number)
         if begin < end:
             run(begin, end, lambda t: slab.step(t - shift))
         begin = end
         corner.event(number)
+        if number == 6:
+            slab.gather()
+            lax.fori_loop(0, t_ref.shape[0] // 8, pick, 0)
         if number >= 4:
             v = number - 4
             corner.complete(v)
@@ -420,7 +442,6 @@
     corner.complete(3)
     for k in range(2):
         pass_share(k, 3).start()
-    slab.gather()
     for v in range(4):
         torus.complete(v)
     for v in range(4):
@@ -433,31 +454,36 @@
     corner.drain()
 
 
-def packed_exchange(index, ptop, ppiece, stop, spiece, x, ticks, owners, ident):
-    vmem = pl.BlockSpec(memory_space=pltpu.VMEM)
+def packed_exchange(index, take, slab, x, ticks, owners, ident):
+    vmem, smem = pl.BlockSpec(memory_space=pltpu.VMEM), pl.BlockSpec(memory_space=pltpu.SMEM)
     z_size, blocks = owners // 2, 2 * (ticks + 1)
-    packed = ticks * ptop.shape[0] + owners * ppiece.shape[0]
+    rows, cols = slab.shape
+    packed = ticks * rows + owners * SLOTS
     torus = (SIDE, SIDE) + x.shape[1:]
     f32 = jnp.float32
-    gs, full, f = pl.pallas_call(
+    full, f, t = pl.pallas_call(
         functools.partial(packed_kernel, ticks, z_size),
         out_shape=(
-            jax.ShapeDtypeStruct((packed, stop.shape[1]), f32),
             jax.ShapeDtypeStruct((ticks,) + torus, f32),
             jax.ShapeDtypeStruct((blocks,) + torus, f32),
+            jax.ShapeDtypeStruct((take.shape[0], cols), f32),
         ),
-        in_specs=[pl.BlockSpec(memory_space=pltpu.SMEM)] + [vmem] * 5,
+        in_specs=[smem, smem, vmem, vmem],
         out_specs=(vmem, vmem, vmem),
         scratch_shapes=[
-            pltpu.VMEM((packed, ptop.shape[1]), f32),
-            pltpu.VMEM((index.shape[0], ptop.shape[1]), f32),
+            pltpu.VMEM((rows, TILE), f32),
+            pltpu.VMEM((SLOTS, TILE), f32),
+            pltpu.VMEM((SLOTS, cols), f32),
+            pltpu.VMEM((packed, cols), f32),
+            pltpu.VMEM((packed, TILE), f32),
+            pltpu.VMEM((index.shape[0] - SLOTS, TILE), f32),
             pltpu.VMEM((blocks,) + x.shape[1:], f32),
             pltpu.SemaphoreType.DMA((2, 4)), pltpu.SemaphoreType.DMA((2, 4)),
         ] + ring_sems(z_size, ticks) * 2 + torus_sems() * 2,
         compiler_params=pltpu.CompilerParams(collective_id=ident, has_side_effects=True),
-    )(index, ptop, ppiece, stop, spiece, x)
+    )(index, take, slab, x)
     width, depth = x.shape[2], SIDE * SIDE * x.shape[1]
-    return gs, full.reshape(ticks, depth, width), f.reshape(blocks, depth, width)
+    return full.reshape(ticks, depth, width), f.reshape(blocks, depth, width), t
 
 
 def invert_tiles(tiles):
@@ -477,7 +503,7 @@
     return inverse
 
 
-def finish_kernel(ticks, f_ref, full_ref, t_ref, base_ref, touched_ref, ints_ref, place_ref, moved_ref,
+def finish_kernel(ticks, f_ref, full_ref, t_ref, base_ref, ints_ref, place_ref, moved_ref,
                   out_ref, inv_ref, u_ref):
     width = f_ref.shape[1]
     tiles = width // TILE
@@ -524,7 +550,7 @@
 
             @pl.when(to >= 0)
             def _():
-                out_ref[pl.ds(to, 1), :] = touched_ref[pl.ds(s, 1), :]
+                out_ref[pl.ds(to, 1), :] = t_ref[pl.ds(ticks * width + s, 1), :]
 
             return carry
 
@@ -544,19 +570,19 @@
         out_ref[...] = out_ref[...] - total.T
 
 
-def finish(ticks, factor, full, t, base, touched, ints, place, moved):
+def finish(ticks, factor, full, t, base, ints, place, moved):
     vmem = pl.BlockSpec(memory_space=pltpu.VMEM)
     width, cols = factor.shape[1], t.shape[1]
     return pl.pallas_call(
         functools.partial(finish_kernel, ticks),
         out_shape=jax.ShapeDtypeStruct(base.shape, jnp.float32),
-        in_specs=[vmem] * 5 + [pl.BlockSpec(memory_space=pltpu.SMEM), vmem, vmem],
+        in_specs=[vmem] * 4 + [pl.BlockSpec(memory_space=pltpu.SMEM), vmem, vmem],
         out_specs=vmem,
         scratch_shapes=[
             pltpu.VMEM((ticks, width, width), jnp.float32), pltpu.VMEM((ticks, cols, width), jnp.float32)
         ],
         compiler_params=pltpu.CompilerParams(vmem_limit_bytes=50 * 1024 * 1024),
-    )(factor, full, t, base, touched, ints, place, moved)
+    )(factor, full, t, base, ints, place, moved)
 
 
 def find(a, b, base):
@@ -583,9 +609,6 @@
     me = lax.axis_index("row")
     src, owner, rank = packs
     top = ticks * width
-    panel_rows = jnp.concatenate(
-        [panels[k] for k in range(ticks)] + [jnp.zeros((rows, 128 - ticks * depth), jnp.float32)], axis=1
-    )
     g = src
     if packed:
         g = jnp.where(owner < ticks, src, top + jnp.minimum(owner * SLOTS + rank, owners * SLOTS - 1))
@@ -624,13 +647,15 @@
         from0, from1 = pos0, pos1
 
     if packed:
-        index = jnp.concatenate([g1, row20, g2, from0, from1])
-        g_slab, full, factor = packed_exchange(
-            index, panel_rows, rows_of(panel_rows, listed), slab, rows_of(slab, listed), x_panels, ticks, owners, 0
-        )
-        base, replaced = slab, rows_of(g_slab, from_slab)
+        index = jnp.concatenate([g1, row20, g2, from0, from1, listed])
+        take = jnp.concatenate([take_t, from_slab])
+        full, factor, t = packed_exchange(index, take, slab, x_panels, ticks, owners, 0)
+        base = slab
         moved = jnp.stack([moved0, moved1] + [touched] * 6).astype(jnp.int32)
     else:
+        panel_rows = jnp.concatenate(
+            [panels[k] for k in range(ticks)] + [jnp.zeros((rows, 128 - ticks * depth), jnp.float32)], axis=1
+        )
         g_panel, full = exchange(panel_rows, x_panels, owners, 1)
 
         def block(index, k):
@@ -647,11 +672,10 @@
         ])
         moved = jnp.zeros((8, rows), jnp.int32)
         place, to = jnp.full((rows,), -1, jnp.int32), jnp.full((PATCH,), -1, jnp.int32)
-        replaced = jnp.zeros((PATCH, cols), jnp.float32)
-    t = rows_of(g_slab, take_t)
+        t = rows_of(g_slab, jnp.concatenate([take_t, jnp.zeros((PATCH,), jnp.int32)]))
     ints = jnp.concatenate([to, jnp.full((8,), me, jnp.int32)])
     place = jnp.broadcast_to(place[None, :], (8, rows))
-    return factor, full, t, base, replaced, ints, place, moved
+    return factor, full, t, base, ints, place, moved
 
 
 def solution(mesh):

time: 139 us -> 130 us (0.935)
  local copies, waits for them, and re-layouts: 17.3 us -> 2.44 us
  Pallas kernels: 112 us -> 117 us
    gather x4 -> x0, local copies, waits for them, and re-layouts: 12 us -> none  [rows_of(): return jnp.take(array, index, axis=0, mode='clip')]
    pallas_call x1, Pallas kernels: 93.4 us -> 97.4 us  [packed_exchange(): pl.pallas_call(functools.partial(packed_kernel, ticks, z_size), out_shape...]
where the time goes in v4:
time: 130 us; the launch traced here: 129 us
  Pallas kernels  117 us (90%)
  other arithmetic  8.87 us (7%)
  local copies, waits for them, and re-layouts  2.44 us (2%)
    pallas_call x1, Pallas kernels, packed_exchange(): pl.pallas_call(functools.partial(packed_kernel, ticks, z_size), out_shape...  97.4 us
    pallas_call x1, Pallas kernels, finish(): pl.pallas_call(functools.partial(finish_kernel, ticks), out_shape=jax.Sha...  19.7 us
    reduce_sum x1, other arithmetic, packing(): return (src, owner, jnp.sum(same.astype(jnp.int32), axis=1))  2.67 us

profile of v4, /device:TPU:64, one launch (start us, length us, event | category | flops | bytes accessed | tf_op | source)
XLA Modules:
  0.0 129.5 jit_solution(2067608856901263806)
XLA Ops:
  0.0 0.8 fusion.24
  0.8 0.3 select_reduce_fusion.11
  1.1 0.6 select_reduce_fusion.10
  1.7 0.5 select_reduce_fusion.7
  2.3 0.1 convert_reduce_fusion.1
  2.5 0.2 select_reduce_fusion.14
  2.7 0.7 reshape.410
  3.4 2.7 %convert_reduce_fusion = s32[1536]{0:T(1024)S(1)} fusion(s32[1536]{0:T(1024)S(1)} %add_select_fusion), kind=kLoop, calls=%fused_computation.57 | loop fusion | flops 11794944 | bytes 12288 | tf_op jit(solution)/shard_map/reduce_sum | solution.py:598
  6.1 1.4 %or_reduce_fusion = pred[]{:T(512)} fusion(pred[3,512]{1,0:T(4,128)(4,1)S(1)} %lt.43, s32[3,512]{1,0:T(4,128)} %param.7), kind=kLoop, calls=%fused_computation.96 | loop fusion | flops 27647 | bytes 7681 | tf_op jit(solution)/shard_map/reduce_and | solution.py:688
  8.1 0.6 convert_element_type.15
  8.8 0.2 select_reduce_fusion.13
  9.0 0.0 copy-start.4
  9.1 0.6 pad_add_fusion.1.take_ref
  9.7 0.7 iota_compare_fusion.3
  10.3 0.0 copy-done.4
  10.3 97.4 %shard_map.39 = (f32[3,4,4,32,512]{4,3,2,1,0:T(8,128)}, f32[8,4,4,32,512]{4,3,2,1,0:T(8,128)}, f32[1664,256]{1,0:T(8,128)}) custom-call(s32[1856]{0:T(1024)} %copy-done.4, s32[1664]{0:T(1024)} %pad_add_fusion.1.take_ref, f32[512,256]{1,0:T(8,128)} %stop_ref.1, f32[3,32,512]{2,1,0:T(8,128)} %bitcast.80), custom_call_target="tpu_custom_call" | custom-call | tf_op jit(solution)/shard_map/pallas_call | solution.py:464
  107.8 20.9 %conditional.1 = (f32[512,256]{1,0:T(8,128)S(1)}) conditional(s32[]{:T(128)} %convert_element_type.13, (f32[3,512,32]{1,2,0:T(8,128)}, s32[3,512]{1,0:T(4,128)}, s32[1536]{0:T(1024)S(1)}, f32[512,256]{1,0:T(8,128)}) %tuple.11, (f32[8,4,4,32,512]{4,3,2,1,0:T(8,128)}, f32[3,4,4,32,512]{4,3,2,1,0:T(8,128)}, pred[128,512]{1,0:T(8,128)(4,1)}, ...), branch_computations={%region_13.20_spmd, %region_20.22_spmd} | conditional | flops 7168900 | bytes 60330456 | solution.py:690
  108.0 1.0 select_reduce_fusion
  109.0 19.7 %branch_1_fun.1 = f32[512,256]{1,0:T(8,128)S(1)} custom-call(f32[8,512,512]{2,1,0:T(8,128)} %bitcast.77, f32[3,512,512]{2,1,0:T(8,128)} %bitcast.79, f32[1664,256]{1,0:T(8,128)} %get-tuple-element.53.t_ref, f32[512,256]{1,0:T(8,128)} %get-tuple-element.54.base_ref, s32[136]{0:T(256)S(1)} %concatenate.15.ints_ref, s32[8,512]{1,0:T(8,128)S(1)} %broadcast_in_dim.203.place_ref, ...), custom_call_target="tpu_custom_call" | custom-call | tf_op jit(solution)/shard_map/cond/branch_1_fun/pallas_call | solution.py:576
  128.7 0.0 copy-start.3
  128.7 0.8 copy-done.3
  (25 shorter events, 0.2 us)
Async XLA Ops:
  9.0 1.3 %copy-start.4 = (s32[1856]{0:T(1024)}, s32[1856]{0:T(1024)S(1)}, u32[]{:S(2)}) copy-start(s32[1856]{0:T(1024)S(1)} %constant_dynamic-update-slice_fusion.index_ref) | copy-start | bytes 22276
  128.7 0.8 copy-start.3

commit v5 on v4

--- a/solution.py
+++ b/solution.py
@@ -14,6 +14,7 @@
 LAG = 4
 SPREAD = 16
 TILE = 128
+DIAGONAL, ACROSS = (0, 1, 4), (2, 5, 6)
 PATCH = 128
 
 
@@ -393,11 +394,24 @@
             rows_ref[pl.ds(at, 1), :] = gp_ref[pl.ds(index_ref[at], 1), :]
         return carry
 
-    lax.fori_loop(0, rows_ref.shape[0] // 8, load, 0)
-    for k in range(ticks):
-        y_ref[k] = gp_ref[pl.ds(k * width, width), :].T[k * depth:(k + 1) * depth]
-    for n, k in ((0, 0), (1, 0), (2, 1)):
-        y_ref[ticks + 1 + n] = rows_ref[pl.ds(n * width, width), :].T[k * depth:(k + 1) * depth]
+    def turn(ref, n, k):
+        return ref[pl.ds(n * width, width), :].T[k * depth:(k + 1) * depth]
+
+    @pl.when(place.core == 0)
+    def _():
+        lax.fori_loop(0, width // 8, load, 0)
+        y_ref[DIAGONAL[0]] = turn(gp_ref, 0, 0)
+        y_ref[DIAGONAL[1]] = turn(gp_ref, 1, 1)
+        y_ref[ACROSS[0]] = turn(rows_ref, 0, 0)
+
+    @pl.when(place.core == 1)
+    def _():
+        lax.fori_loop(width // 8, 3 * width // 8, load, 0)
+        y_ref[DIAGONAL[2]] = turn(gp_ref, 2, 2)
+        y_ref[ACROSS[1]] = turn(rows_ref, 1, 0)
+        y_ref[ACROSS[2]] = turn(rows_ref, 2, 1)
+
+    lax.fori_loop(3 * width // 8, rows_ref.shape[0] // 8, load, 0)
     patches = rows_ref[pl.ds(3 * width, 2 * PATCH), :].T
     zeros = jnp.zeros((depth, width - 2 * PATCH), jnp.float32)
     y_ref[mine + ticks] = jnp.concatenate([patches[:depth, :PATCH], patches[depth:2 * depth, PATCH:], zeros], axis=1)
@@ -503,35 +517,38 @@
     return inverse
 
 
-def finish_kernel(ticks, f_ref, full_ref, t_ref, base_ref, ints_ref, place_ref, moved_ref,
+def finish_kernel(ticks, together, f_ref, full_ref, t_ref, base_ref, ints_ref, place_ref, moved_ref,
                   out_ref, inv_ref, u_ref):
     width = f_ref.shape[1]
     tiles = width // TILE
     inv_ref[...] = jnp.zeros_like(inv_ref)
 
-    def invert(b, carry):
-        spots = [pl.ds(j * TILE, TILE) for j in range(tiles)]
-        for spot, one in zip(spots, invert_tiles([f_ref[b, spot, spot] for spot in spots])):
+    def invert(bs):
+        spots = [(b, pl.ds(j * TILE, TILE)) for b in bs for j in range(tiles)]
+        inverses = invert_tiles([f_ref[b + 2 * (b // 2), spot, spot] for b, spot in spots])
+        for (b, spot), one in zip(spots, inverses):
             inv_ref[b, spot, spot] = one
-        return carry
-
-    lax.fori_loop(0, ticks, invert, 0)
+
+    if together:
+        invert(range(ticks))
+    else:
+        run(0, ticks, lambda b: invert([b]))
     size = TILE
     while size < width:
         spots = [
             (b, pl.ds(low, size), pl.ds(low + size, size))
             for b in range(ticks) for low in range(0, width, 2 * size)
         ]
-        half = [mul(f_ref[b, near, far], inv_ref[b, far, far]) for b, near, far in spots]
+        half = [mul(f_ref[DIAGONAL[b], near, far], inv_ref[b, far, far]) for b, near, far in spots]
         for (b, near, far), tile in zip(spots, half):
             inv_ref[b, near, far] = -mul(inv_ref[b, near, near], tile)
         size *= 2
 
-    off = ticks + 1
+    off = 0
     for b in range(ticks):
         rhs = t_ref[pl.ds(b * width, width), :].T
         for j in range(b):
-            rhs = rhs - mul(u_ref[j], f_ref[off])
+            rhs = rhs - mul(u_ref[j], f_ref[ACROSS[off]])
             off += 1
         u_ref[b] = mul(rhs, inv_ref[b])
 
@@ -570,11 +587,11 @@
         out_ref[...] = out_ref[...] - total.T
 
 
-def finish(ticks, factor, full, t, base, ints, place, moved):
+def finish(ticks, together, factor, full, t, base, ints, place, moved):
     vmem = pl.BlockSpec(memory_space=pltpu.VMEM)
     width, cols = factor.shape[1], t.shape[1]
     return pl.pallas_call(
-        functools.partial(finish_kernel, ticks),
+        functools.partial(finish_kernel, ticks, together),
         out_shape=jax.ShapeDtypeStruct(base.shape, jnp.float32),
         in_specs=[vmem] * 4 + [pl.BlockSpec(memory_space=pltpu.SMEM), vmem, vmem],
         out_specs=vmem,
@@ -661,8 +678,9 @@
         def block(index, k):
             return rows_of(g_panel, index)[:, k * depth:(k + 1) * depth].T
 
-        corner = [g_panel[k * width:(k + 1) * width, k * depth:(k + 1) * depth].T for k in range(ticks)]
-        corner += [block(from0, 0), block(g1, 0), block(row20, 0), block(g2, 1), block(from1, 1)]
+        lower = [g_panel[k * width:(k + 1) * width, k * depth:(k + 1) * depth].T for k in range(ticks)]
+        corner = [lower[0], lower[1], block(g1, 0), block(from0, 0)]
+        corner += [lower[2], block(row20, 0), block(g2, 1), block(from1, 1)]
         g_slab, factor = exchange(slab, jnp.stack(corner), owners, 2)
         base = jnp.where(touched[:, None], rows_of(g_slab, orig), slab)
         full = jnp.stack([
@@ -689,8 +707,8 @@
         ready = update(True, owners, slab, panels, pivots, packs)
         return lax.cond(
             fits,
-            lambda ready, rest: finish(ticks, *ready),
-            lambda ready, rest: finish(ticks, *update(False, owners, *rest)),
+            lambda ready, rest: finish(ticks, True, *ready),
+            lambda ready, rest: finish(ticks, False, *update(False, owners, *rest)),
             ready, (slab, panels, pivots, packs),
         )
 

time: 130 us -> 126 us (0.969)
  the two profiles are of different devices: /device:TPU:64 before, /device:TPU:289 now
where the time goes in v5:
time: 126 us
  Pallas kernels  113 us (90%)
  other arithmetic  8.87 us (7%)
  local copies, waits for them, and re-layouts  2.44 us (2%)
    pallas_call x1, Pallas kernels, packed_exchange(): pl.pallas_call(functools.partial(packed_kernel, ticks, z_size), out_shape...  96.6 us
    pallas_call x1, Pallas kernels, finish(): pl.pallas_call(functools.partial(finish_kernel, ticks, together), out_sha...  16.7 us
    reduce_sum x1, other arithmetic, packing(): return (src, owner, jnp.sum(same.astype(jnp.int32), axis=1))  2.67 us

profile of v5, /device:TPU:289, one launch (start us, length us, event | category | flops | bytes accessed | tf_op | source)
XLA Modules:
  0.0 125.7 jit_solution(10841634835965192854)
XLA Ops:
  0.0 0.8 fusion.24
  0.8 0.3 select_reduce_fusion.11
  1.1 0.6 select_reduce_fusion.10
  1.7 0.5 select_reduce_fusion.7
  2.3 0.1 convert_reduce_fusion.1
  2.5 0.2 select_reduce_fusion.14
  2.7 0.7 reshape.410
  3.4 2.7 %convert_reduce_fusion = s32[1536]{0:T(1024)S(1)} fusion(s32[1536]{0:T(1024)S(1)} %add_select_fusion), kind=kLoop, calls=%fused_computation.57 | loop fusion | flops 11794944 | bytes 12288 | tf_op jit(solution)/shard_map/reduce_sum | solution.py:615
  6.1 1.4 %or_reduce_fusion = pred[]{:T(512)} fusion(pred[3,512]{1,0:T(4,128)(4,1)S(1)} %lt.43, s32[3,512]{1,0:T(4,128)} %param.7), kind=kLoop, calls=%fused_computation.96 | loop fusion | flops 27647 | bytes 7681 | tf_op jit(solution)/shard_map/reduce_and | solution.py:706
  8.1 0.6 convert_element_type.15
  8.8 0.2 select_reduce_fusion.13
  9.0 0.0 copy-start.4
  9.1 0.6 pad_add_fusion.1.take_ref
  9.7 0.7 iota_compare_fusion.3
  10.3 0.0 copy-done.4
  10.3 96.6 %shard_map.39 = (f32[3,4,4,32,512]{4,3,2,1,0:T(8,128)}, f32[8,4,4,32,512]{4,3,2,1,0:T(8,128)}, f32[1664,256]{1,0:T(8,128)}) custom-call(s32[1856]{0:T(1024)} %copy-done.4, s32[1664]{0:T(1024)} %pad_add_fusion.1.take_ref, f32[512,256]{1,0:T(8,128)} %stop_ref.1, f32[3,32,512]{2,1,0:T(8,128)} %bitcast.80), custom_call_target="tpu_custom_call" | custom-call | tf_op jit(solution)/shard_map/pallas_call | solution.py:478
  107.0 17.9 %conditional.1 = (f32[512,256]{1,0:T(8,128)S(1)}) conditional(s32[]{:T(128)} %convert_element_type.13, (f32[3,512,32]{1,2,0:T(8,128)}, s32[1536]{0:T(1024)S(1)}, s32[3,512]{1,0:T(4,128)}, f32[512,256]{1,0:T(8,128)}) %tuple.11, (f32[8,4,4,32,512]{4,3,2,1,0:T(8,128)}, f32[3,4,4,32,512]{4,3,2,1,0:T(8,128)}, pred[128,512]{1,0:T(8,128)(4,1)}, ...), branch_computations={%region_13.20_spmd, %region_20.22_spmd} | conditional | flops 7168900 | bytes 60330456 | solution.py:708
  107.2 1.0 select_reduce_fusion
  108.2 16.7 %branch_1_fun.1 = f32[512,256]{1,0:T(8,128)S(1)} custom-call(f32[8,512,512]{2,1,0:T(8,128)} %bitcast.77, f32[3,512,512]{2,1,0:T(8,128)} %bitcast.79, f32[1664,256]{1,0:T(8,128)} %get-tuple-element.53.t_ref, f32[512,256]{1,0:T(8,128)} %get-tuple-element.54.base_ref, s32[136]{0:T(256)S(1)} %concatenate.15.ints_ref, s32[8,512]{1,0:T(8,128)S(1)} %broadcast_in_dim.203.place_ref, ...), custom_call_target="tpu_custom_call" | custom-call | tf_op jit(solution)/shard_map/cond/branch_1_fun/pallas_call | solution.py:593
  124.9 0.0 copy-start.3
  124.9 0.8 copy-done.3
  (25 shorter events, 0.2 us)
Async XLA Ops:
  9.0 1.3 %copy-start.4 = (s32[1856]{0:T(1024)}, s32[1856]{0:T(1024)S(1)}, u32[]{:S(2)}) copy-start(s32[1856]{0:T(1024)S(1)} %constant_dynamic-update-slice_fusion.index_ref) | copy-start | bytes 22276
  124.9 0.8 copy-start.3
